TPU v7x, 32 devices: a whole 2x2x4 slice. The times are simulated.
32 devices in a mesh: view: 4 (over x, core), bx: 4 (over z), by: 2 (over y).
Axes of the slice: x: 2, y: 2, z: 4, core: 2. Of those that a mesh axis runs over, the one named last changes fastest.
Arguments:
- estimate: float32 [256, 32, 128], P('bx', 'by'), may hold values from 0.5 to 2
- observed: float32 [4, 2048, 512], P('view', ('bx', 'by')), may hold values from 0.25 to 4
- destination: int32 [4, 2048, 1], P('view', ('bx', 'by')), may hold values from 0 to 7; in each aligned block of 256 rows (0 to 255, 256 to 511, ..., all dimensions but the last counted through in order) at most 64 rows name the same one
- slot_index: int32 [4, 2048], P('view', ('bx', 'by')), may hold values from 0 to 255
- valid_count: int32 [4, 2048], P('view', ('bx', 'by')), may hold values from 32 to 128
- blend_weight: float32 [4, 2048], P('view', ('bx', 'by')), may hold values from 0.2 to 1
- kernel_x: float32 [4, 17], P('view'), may hold values from 0.1 to 1
- kernel_y: float32 [4, 17], P('view'), may hold values from 0.1 to 1
- kernel_z: float32 [4, 33], P('view'), may hold values from 0.1 to 1
Outputs:
- updated: float32 [256, 32, 128], P('bx', 'by')
Inputs may be any that keep to these rules, and one draw needn't show every extreme that they name: `destination`: in each view, the 256 rows of one device name no brick more than 64 times, a bound that some block reaches.
All inputs are finite; a program needn't handle non-finite values.
Results may differ from a plain program's by a relative error of at most 0.0001.
Values sent between devices are 32-bit elements; how exact they have to be, the bound alone decides.
No kernel may reach another device: no remote copies, remote signals or barrier semaphores. Data moves between devices by JAX's collectives and lax.ppermute only.
A program may use at most 64 MiB of HBM per device.

v0:
```python
import jax
import jax.numpy as jnp
from jax import lax
from jax.experimental import pallas as pl
from jax.experimental.pallas import tpu as pltpu
from jax.sharding import PartitionSpec as P


R = 8
RZ = 16
YP = 4
PV = 512
SLOTS = 256
PIECES = 256
CX = 64
CY = 16
CZ = 128
PRIOR_WEIGHT = 0.5
F32 = jnp.float32
BF16 = jnp.bfloat16
VM = pl.BlockSpec(memory_space=pltpu.VMEM)
SM = pl.BlockSpec(memory_space=pltpu.SMEM)
ANY = pl.BlockSpec(memory_space=pl.ANY)
HB = pl.BlockSpec(memory_space=pltpu.HBM)
HX = CX // 2
HY = CY // 2
XE = CX + 2 * R
TAPS = 2 * R + 1
ROWS = 24
PACK_LIMIT = 32 << 20
BLUR_LIMIT = 32 << 20
GROUP = 64
CHUNK = YP * GROUP + 8


def call(
    kernel,
    outs,
    scratch=(),
    in_specs=None,
    out_specs=None,
    aliases=None,
    limit=32 << 20,
    flops=1 << 22,
    moved=1 << 20,
):
    shapes = [o if hasattr(o, "dtype") else jax.ShapeDtypeStruct(o, F32) for o in outs]
    return pl.pallas_call(
        kernel,
        out_shape=shapes,
        in_specs=in_specs,
        out_specs=out_specs or [VM] * len(outs),
        scratch_shapes=list(scratch),
        input_output_aliases=aliases or {},
        compiler_params=pltpu.CompilerParams(vmem_limit_bytes=limit),
        cost_estimate=pl.CostEstimate(flops=flops, bytes_accessed=moved, transcendentals=0),
    )


def three(x):
    high = x.astype(BF16)
    rest = x - high.astype(F32)
    mid = rest.astype(BF16)
    return high, mid, (rest - mid.astype(F32)).astype(BF16)


def two(x):
    high = x.astype(BF16)
    return high, (x - high.astype(F32)).astype(BF16)


def iota(shape, dim):
    return lax.broadcasted_iota(jnp.int32, shape, dim)


def mm(a, b):
    return jnp.dot(a, b, preferred_element_type=F32)


def pack_kernel(*refs):
    sources, outs, token, held, sems = refs[:5], refs[5:-7], refs[-7], refs[-6:-1], refs[-1]
    bricks = len(outs)
    token[...] = jnp.zeros((8, CZ), F32)
    copies = [
        pltpu.make_async_copy(source, to, sems.at[i])
        for i, (source, to) in enumerate(zip(sources, held))
    ]
    for copy in copies:
        copy.start()
    observed, target, slot, count, weight = held
    for copy in copies[1:]:
        copy.wait()
    me = lax.axis_index("bx") * lax.axis_size("by") + lax.axis_index("by")
    goal = target[...] ^ me
    member = (iota((bricks, PIECES), 0) == goal).astype(F32)
    upto = (iota((PIECES, PIECES), 0) <= iota((PIECES, PIECES), 1)).astype(F32)
    ranks = mm(member.astype(BF16), upto.astype(BF16))
    rank = jnp.sum(member * ranks, axis=0, keepdims=True).astype(jnp.int32) - 1
    place = goal * GROUP + rank
    rows = bricks * GROUP
    pick = (iota((rows, PIECES), 0) == place).astype(F32).astype(BF16)
    keep = jnp.where(iota((CZ, PIECES), 0) < count[...], weight[...], 0.0).T
    copies[0].wait()
    weighted = observed[...] * jnp.concatenate([keep] * YP, axis=1)
    packed = sum(mm(pick, part) for part in three(weighted))
    parts = [p.astype(F32) for p in three(weight[...])]
    table = jnp.concatenate(
        [slot[...].astype(F32), count[...].astype(F32)] + parts + [jnp.zeros((3, PIECES), F32)],
        axis=0,
    )
    meta = lax.dot_general(
        table.astype(BF16), pick, (((1,), (1,)), ((), ())), preferred_element_type=F32
    )
    wide = jnp.concatenate(
        [meta[0:2], meta[2:3] + meta[3:4] + meta[4:5], jnp.zeros((5, rows), F32)], axis=0
    )
    lane = iota((8, CZ), 1)
    for s in range(bricks):
        for j in range(YP):
            outs[s][j * GROUP : (j + 1) * GROUP, :] = packed[
                s * GROUP : (s + 1) * GROUP, j * CZ : (j + 1) * CZ
            ]
        pair = wide[:, (s // 2) * CZ : (s // 2 + 1) * CZ]
        if s % 2:
            pair = pltpu.roll(pair, GROUP, 1)
        outs[s][YP * GROUP :, :] = jnp.where(lane < GROUP, pair, 0.0)


def sides():
    odd_x = lax.axis_index("bx") % 2
    odd_y = lax.axis_index("by") % 2
    return odd_x, odd_y


def put_edges(volume, outs):
    odd_x, odd_y = sides()
    at_x = [pl.multiple_of((1 - odd_x) * (CX - R), R), pl.multiple_of(odd_x * (CX - R), R)]
    at_y = [(1 - odd_y) * (CY - R), odd_y * (CY - R)]
    for phase in range((len(outs) - 2) // 3):
        whole, first, second = outs[3 * phase : 3 * phase + 3]
        rows = pl.ds(at_y[phase], R)
        whole[...] = volume[rows]
        first[...] = volume[rows, pl.ds(at_x[0], R), :]
        second[...] = volume[rows, pl.ds(at_x[1], R), :]
    outs[-2][...] = volume[:, pl.ds(at_x[0], R), :]
    outs[-1][...] = volume[:, pl.ds(at_x[1], R), :]


def turn_kernel(estimate, after, turned, *edges):
    for y in range(CY):
        turned[y] = estimate[pl.ds(y, CX, stride=CY), :]
    put_edges(turned, edges)


def total(kernel, taps):
    acc = kernel[0, 0]
    for i in range(1, taps):
        acc = acc + kernel[0, i]
    return acc


def make_bands(kx, ky, kz, *outs):
    ztaps = 2 * RZ + 1
    for reverse in range(2):
        band_x, band_z, taps = outs[3 * reverse : 3 * reverse + 3]
        col, row = iota((CX, 3 * XE), 1), iota((CX, 3 * XE), 0)
        block = jnp.where(col >= 2 * XE, 2, jnp.where(col >= XE, 1, 0))
        gap = col - block * XE - row
        band = jnp.zeros((CX, 3 * XE), F32)
        for i in range(TAPS):
            band = jnp.where(gap == i, kx[0, TAPS - 1 - i if reverse else i], band)
        high, low = two(band / total(kx, TAPS))
        band_x[...] = jnp.where(block == 1, low.astype(F32), high.astype(F32)).astype(BF16)
        gap = iota((CZ, CZ), 0) - iota((CZ, CZ), 1) + RZ
        band = jnp.zeros((CZ, CZ), F32)
        for i in range(ztaps):
            band = jnp.where(gap == i, kz[0, ztaps - 1 - i if reverse else i], band)
        high, low = two(band / total(kz, ztaps))
        band_z[...] = jnp.concatenate([high, low, high], axis=0)
        row = iota((ROWS, CZ), 0)
        table = jnp.zeros((ROWS, CZ), F32)
        for i in range(TAPS):
            table = jnp.where(row == i, ky[0, TAPS - 1 - i if reverse else i], table)
        taps[...] = table / total(ky, TAPS)


def smear_x(padded, count, band_x, lines, base):
    for y in range(0, count, 2):
        stack = []
        for k in range(2):
            high, low = two(padded[y + k])
            stack.append(jnp.concatenate([high, high, low], axis=0))
        both = mm(band_x[...], jnp.concatenate(stack, axis=1))
        lines[base + y] = both[:, :CZ]
        lines[base + y + 1] = both[:, CZ:]


def smear_yz(lines, base, taps, band_z, held):
    tap = [taps[i : i + 1, :] for i in range(TAPS)]

    def tile(t, carry):
        at = pl.ds(pl.multiple_of(t * 8, 8), 8)
        acc = [None] * HY
        for i in range(HY + 2 * R):
            value = lines[base + i, at, :]
            for y in range(HY):
                if 0 <= i - y < TAPS:
                    term = tap[i - y] * value
                    acc[y] = term if acc[y] is None else acc[y] + term
        for y in range(HY):
            held[y, at, :] = acc[y]
        return carry

    lax.fori_loop(0, CX // 8, tile, 0)
    high, low = two(held[...].reshape(HY * CX, CZ))
    result = mm(jnp.concatenate([high, high, low], axis=1), band_z[...])
    return [result[y * CX : (y + 1) * CX] for y in range(HY)]


def put_x(own, xa, xb, padded, count):
    odd_x, _ = sides()
    padded[:count, R : R + CX, :] = own[...]
    padded[:count, pl.ds(pl.multiple_of((1 - odd_x) * (CX + R), R), R), :] = xa[...]
    padded[:count, pl.ds(pl.multiple_of(odd_x * (CX + R), R), R), :] = xb[...]


def far_lines(own, x_halos, y_halos, band_x, padded, lines):
    _, odd_y = sides()
    put_x(own, *x_halos, padded, CY)
    smear_x(padded, CY, band_x, lines, R)
    far = (CY + R) * odd_y
    if y_halos:
        put_x(*y_halos, padded, R)
        smear_x(padded, R, band_x, lines, far)
    else:
        lines[pl.ds(far, R)] = jnp.zeros((R, CX, CZ), F32)


def near_lines(y_halos, band_x, padded, lines):
    _, odd_y = sides()
    put_x(*y_halos, padded, R)
    smear_x(padded, R, band_x, lines, (CY + R) * (1 - odd_y))


def blur_kernel(own, *refs):
    halos, (kx, ky, kz, out, *bands) = refs[:-13], refs[-13:]
    band_x, band_z, taps, padded, lines, held = bands[3:]
    make_bands(kx, ky, kz, *bands[3:6], *bands[:3])
    far_lines(own, halos[-2:], halos[3:-2], band_x, padded, lines)
    near_lines(halos[:3], band_x, padded, lines)
    for start in range(0, CY, HY):
        for y, value in enumerate(smear_yz(lines, start, taps, band_z, held)):
            out[start + y] = value


def put_quarters(values, mine, other, whole):
    core = lax.axis_index("view") % 2
    for y in range(HY):
        whole[pl.ds(y, CX, stride=HY), :] = values[y]
    rows = HX * HY
    other[...] = whole[pl.ds(pl.multiple_of((1 - core) * rows, rows), rows), :]
    mine[...] = whole[pl.ds(pl.multiple_of(core * rows, rows), rows), :]


def far_kernel(own, *refs):
    ins, (mine, other, lines, padded, held, whole) = refs[:-6], refs[-6:]
    halos, (band_x, band_z, taps) = ins[:-3], ins[-3:]
    _, odd_y = sides()
    far_lines(own, halos[-2:], halos[:-2], band_x, padded, lines)
    values = smear_yz(lines, HY * odd_y, taps, band_z, held)
    put_quarters(values, mine, other, whole)


def near_kernel(after, before, *refs):
    halos, (band_x, band_z, taps, mine, other, padded, held, whole, lines) = refs[:3], refs[3:]
    _, odd_y = sides()
    lines[R : R + CY] = before[R : R + CY]
    near_lines(halos, band_x, padded, lines)
    values = smear_yz(lines, HY * (1 - odd_y), taps, band_z, held)
    put_quarters(values, mine, other, whole)


def ratio_kernel(chunks, *refs):
    parts, blurred = refs[:chunks], refs[chunks]
    ratio, *edges = refs[chunks + 1 :]
    rows = chunks * GROUP
    metas = []
    for c in range(0, chunks, 2):
        odd = pltpu.roll(parts[c + 1][YP * GROUP :, :], GROUP, 1)
        metas.append(parts[c][YP * GROUP :, :] + odd)
    meta = jnp.concatenate(metas, axis=1)
    slot, count, weight = meta[0:1].astype(jnp.int32), meta[1:2].astype(jnp.int32), meta[2:3]
    key = (slot & (YP - 1)) * CX + (slot >> 2)
    chooser = (iota((SLOTS, rows), 0) == key).astype(F32).astype(BF16)
    keep = jnp.where(iota((CZ, rows), 0) < count, weight, 0.0).T

    def gathered(values):
        return sum(mm(chooser, part) for part in three(values))

    cover = gathered(keep)
    for j in range(0, YP, 2):
        values = jnp.concatenate(
            [
                jnp.concatenate([p[k * GROUP : (k + 1) * GROUP, :] for p in parts], axis=0)
                for k in (j, j + 1)
            ],
            axis=1,
        )
        data = gathered(values)
        for q in range(CY // YP):
            at = slice(q * CX, (q + 1) * CX)
            for k in range(2):
                y = YP * q + j + k
                base = blurred[y]
                ratio[y] = (data[at, k * CZ : (k + 1) * CZ] + PRIOR_WEIGHT * base) / (
                    (cover[at] + PRIOR_WEIGHT) * base
                )
    put_edges(ratio, edges)


def store_kernel(parts, *refs):
    ins, out, sems = refs[: len(parts)], refs[-2], refs[-1]
    core, (_, odd_y) = lax.axis_index("view") % 2, sides()
    copies = []
    for i, (part, near) in enumerate(parts):
        x = pl.multiple_of(HX * (core if part == 0 else 1 - core), HX)
        y = pl.multiple_of(HY * (1 - odd_y if near else odd_y), HY)
        to = out.at[pl.ds(x, HX), pl.ds(y, HY), :]
        copies.append(pltpu.make_async_copy(ins[i], to, sems.at[i]))
        copies[-1].start()
    for copy in copies:
        copy.wait()


def store(parts, values, before):
    def kernel(*refs):
        store_kernel(parts, *refs)

    values = [value.reshape(HX, HY, CZ) for value in values]
    specs, aliases = [VM] * len(values), {}
    if before is not None:
        values.append(before)
        specs.append(ANY)
        aliases = {len(parts): 0}
    sems = [pltpu.SemaphoreType.DMA((len(parts),))]
    return call(kernel, [(CX, CY, CZ)], sems, specs, [ANY], aliases)(*values)[0]


def swap(x, axis, mask):
    return lax.ppermute(x, axis, [(i, i ^ mask) for i in range(lax.axis_size(axis))])


def pairs(axis):
    count = lax.axis_size(axis)
    first = [(i, i ^ 1) for i in range(count) if i ^ 1 < count]
    second = [(i, ((i + 1) ^ 1) - 1) for i in range(count)]
    second = [(i, k) for i, k in second if 0 <= k < count]
    return [first] + ([second] if second else [])


def halo_pairs():
    x_pairs, y_pairs, wide = pairs("bx"), pairs("by"), lax.axis_size("by")
    x_pairs = x_pairs + [[]] * (2 - len(x_pairs))
    out = []
    for ys in y_pairs:
        out.append(("by", ys))
        for xs in x_pairs:
            moves = [(a * wide + c, b * wide + d) for a, b in xs for c, d in ys]
            out.append((("bx", "by"), moves))
    return out + [("bx", xs) for xs in x_pairs]


def halo(edges):
    got = []
    for edge, (axis, moves) in zip(edges, halo_pairs()):
        got.append(lax.ppermute(edge, axis, moves) if moves else jnp.zeros_like(edge))
    return got


def generic_exchange(bricks, observed, target, slot, count, weight):
    capacity = max(4, 2 * PIECES // bricks)
    member = (target[:, None] == jnp.arange(bricks)[None, :]).astype(jnp.int32)
    slot_rank = jnp.sum((jnp.cumsum(member, axis=0) - 1) * member, axis=1)
    place = target * capacity + slot_rank
    keep = jnp.where(jnp.arange(CZ)[None, :] < count[:, None], weight[:, None], 0.0)
    weighted = (observed.reshape(-1, YP, CZ) * keep[:, None, :]).reshape(-1, PV)
    facts = jnp.stack([slot.astype(F32), count.astype(F32), weight], axis=1)
    rows = jnp.zeros((bricks * capacity, PV), F32).at[place].set(weighted)
    facts = jnp.zeros((bricks * capacity, 3), F32).at[place].set(facts)

    def exchange(x):
        x = x.reshape(bricks, capacity, -1)
        return lax.all_to_all(x, ("bx", "by"), split_axis=0, concat_axis=0, tiled=True)

    chunks = bricks * capacity // GROUP
    rows = exchange(rows).reshape(chunks, GROUP, YP, CZ).transpose(0, 2, 1, 3)
    facts = exchange(facts).reshape(chunks, GROUP, 3).transpose(0, 2, 1)
    facts = jnp.pad(facts, ((0, 0), (0, 5), (0, CZ - GROUP)))
    both = jnp.concatenate([rows.reshape(chunks, YP * GROUP, CZ), facts], axis=1)
    return [both[c] for c in range(chunks)]


def local(
    estimate,
    observed,
    destination,
    slot_index,
    valid_count,
    blend_weight,
    kernel_x,
    kernel_y,
    kernel_z,
):
    count_bx, count_by = lax.axis_size("bx"), lax.axis_size("by")
    bricks = count_bx * count_by
    phases = len(pairs("by"))
    flat = estimate.reshape(CX * CY, CZ)
    edge_shapes = [(R, CX, CZ), (R, R, CZ), (R, R, CZ)] * phases + [(CY, R, CZ)] * 2
    brick, quarter, lines = (CY, CX, CZ), (HX * HY, CZ), (CY + 2 * R, CX, CZ)
    padded, held = pltpu.VMEM((CY, XE, CZ), F32), pltpu.VMEM((HY, CX, CZ), F32)
    whole = pltpu.VMEM((CX * HY, CZ), F32)

    if bricks * GROUP == 2 * PIECES:
        room = [pltpu.VMEM((PIECES, PV), F32)]
        room += [pltpu.VMEM((1, PIECES), jnp.int32)] * 3 + [pltpu.VMEM((1, PIECES), F32)]
        room.append(pltpu.SemaphoreType.DMA((5,)))
        shapes = [(CHUNK, CZ)] * bricks + [(8, CZ)]
        *packed, token = call(pack_kernel, shapes, room, [HB] * 5, limit=PACK_LIMIT)(
            *[
                pltpu.with_memory_space_constraint(x, pltpu.HBM)
                for x in (
                    observed[0],
                    destination.reshape(1, PIECES),
                    slot_index,
                    valid_count,
                    blend_weight,
                )
            ]
        )
        chunks = [packed[0]]
        for s in sorted(range(1, bricks), reverse=True):
            pair = [(d, d ^ s) for d in range(bricks)]
            chunks.append(lax.ppermute(packed[s], ("bx", "by"), pair))
    else:
        token = jnp.zeros((8, CZ), F32)
        chunks = generic_exchange(
            bricks,
            observed[0],
            destination[0, :, 0],
            slot_index[0],
            valid_count[0],
            blend_weight[0],
        )

    turned, *edges = call(turn_kernel, [brick] + edge_shapes, in_specs=[VM, ANY])(flat, token)
    around = halo(edges)
    bands = [((CX, 3 * XE), BF16), ((3 * CZ, CZ), BF16), ((ROWS, CZ), F32)]
    work = [pltpu.VMEM(*band) for band in bands] + [padded, pltpu.VMEM(lines, F32), held]
    shapes = [brick] + [jax.ShapeDtypeStruct(*band) for band in bands]
    specs = [VM] * (len(around) + 1) + [SM] * 3
    blurred, *bands = call(blur_kernel, shapes, work, specs, limit=BLUR_LIMIT)(
        turned, *around, kernel_x, kernel_y, kernel_z
    )

    def ratios(*refs):
        ratio_kernel(len(chunks), *refs)

    ratio, *edges = call(ratios, [brick] + edge_shapes, in_specs=[VM] * (len(chunks) + 1))(
        *chunks, blurred
    )
    around = halo(edges)
    near_halos, far_halos = around[:3], around[3:]
    mine, other, before = call(
        far_kernel, [quarter, quarter, lines], [padded, held, whole], [VM] * (len(far_halos) + 4)
    )(ratio, *far_halos, *bands)
    core, odd_y = lax.axis_index("view") % 2, lax.axis_index("by") % 2

    def paired(mine, other):
        return mine * swap(other, "view", 1)

    def product(mine, start, estimate):
        across = swap(mine, "view", 2)
        own = lax.dynamic_slice(estimate, (core * HX, start * HY, 0), (HX, HY, CZ))
        mine = mine * across * own.reshape(HX * HY, CZ)
        return mine, swap(mine, "view", 1)

    mine = paired(mine, other)
    work = [padded, held, whole, pltpu.VMEM(lines, F32)]
    near = call(near_kernel, [quarter, quarter], work, [ANY] + [VM] * 7)(
        mine, before, *near_halos, *bands
    )
    far_mine, far_other = product(mine, odd_y, estimate)
    updated = store([(0, False), (1, False)], [far_mine, far_other], None)
    estimate, far_mine = lax.optimization_barrier((estimate, far_mine))
    near_mine, near_other = product(paired(*near), 1 - odd_y, estimate)
    updated = store([(0, True)], [near_mine], updated)
    return store([(1, True)], [near_other], updated)


def solution(mesh):
    placed = (
        P("bx", "by", None),
        P("view", ("bx", "by"), None),
        P("view", ("bx", "by"), None),
        P("view", ("bx", "by")),
        P("view", ("bx", "by")),
        P("view", ("bx", "by")),
        P("view", None),
        P("view", None),
        P("view", None),
    )

    return jax.shard_map(
        local, mesh=mesh, in_specs=placed, out_specs=P("bx", "by", None), check_vma=False
    )
```

profile of v0, /device:TPU:9, one launch (start us, length us, event | category | flops | bytes accessed | tf_op | source)
XLA Modules:
  0.0 70.5 jit_solution(1172094183660213758)
XLA Ops:
  0.0 1.9 %shard_map.91 = (f32[264,128]{1,0:T(8,128)S(1)}, f32[264,128]{1,0:T(8,128)S(1)}, f32[264,128]{1,0:T(8,128)S(1)}, f32[264,128]{1,0:T(8,128)S(1)}, f32[264,128]{1,...) custom-call(f32[256,512]{1,0:T(8,128)} %bitcast.16, ...), custom_call_target="tpu_custom_call" | custom-call | flops 4194304 | bytes 1048576 | tf_op jit(solution)/shard_map/pallas_call | solution.py:428
  2.2 1.3 %collective-permute-start.7 = (f32[8,64,128]{2,1,0:T(8,128)S(1)}, f32[8,64,128]{2,1,0:T(8,128)S(1)}, u32[]{:S(2)}, u32[]{:S(2)}) collective-permute-start(f32[8,64,128]{2,1,0:T(8,128)S(1)} %get-tuple-element.46), channel_id=1, source_target_pairs={{0,1},{1,0},{2,3},{3,2},{4,5},{5,4},{6,7},{7,6},{8,9},{9,8},{10,11... | collective-permute-start | bytes 786440 | tf_op jit(solution)/shard_map/ppermute | solution.py:376
  3.5 1.2 %collective-permute-start = (f32[264,128]{1,0:T(8,128)S(1)}, f32[264,128]{1,0:T(8,128)S(1)}, u32[]{:S(2)}, u32[]{:S(2)}) collective-permute-start(f32[264,128]{1,0:T(8,128)S(1)} %get-tuple-element.37), channel_id=1, source_target_pairs={{0,7},{1,6},{2,5},{3,4},{4,3},{5,2},{6,1},{7,0},{8,15},{9,14},{10,... | collective-permute-start | bytes 405512 | tf_op jit(solution)/shard_map/ppermute | solution.py:443
  4.9 3.0 %collective-permute-start.8 = (f32[8,8,128]{2,1,0:T(8,128)S(1)}, f32[8,8,128]{2,1,0:T(8,128)S(1)}, u32[]{:S(2)}, u32[]{:S(2)}) collective-permute-start(f32[8,8,128]{2,1,0:T(8,128)S(1)} %get-tuple-element.47), channel_id=1, source_target_pairs={{0,3},{1,2},{2,1},{3,0},{4,7},{5,6},{6,5},{7,4},{8,11},{9,10},{10,... | collective-permute-start | bytes 98312 | tf_op jit(solution)/shard_map/ppermute | solution.py:376
  7.9 4.2 %collective-permute-start.9 = (f32[8,8,128]{2,1,0:T(8,128)S(1)}, f32[8,8,128]{2,1,0:T(8,128)S(1)}, u32[]{:S(2)}, u32[]{:S(2)}) collective-permute-start(f32[8,8,128]{2,1,0:T(8,128)S(1)} %get-tuple-element.48), channel_id=1, source_target_pairs={{2,5},{3,4},{4,3},{5,2},{10,13},{11,12},{12,11},{13,10},{18,21},{1... | collective-permute-start | bytes 98312 | tf_op jit(solution)/shard_map/ppermute | solution.py:376
  12.1 2.3 %collective-permute-done.8.refs_1_ = f32[8,8,128]{2,1,0:T(8,128)S(1)} collective-permute-done((f32[8,8,128]{2,1,0:T(8,128)S(1)}, f32[8,8,128]{2,1,0:T(8,128)S(1)}, u32[]{:S(2)}, u32[]{:S(2)}) %collective-permute-start.8) | collective-permute-done | bytes 32800 | tf_op jit(solution)/shard_map/ppermute | solution.py:376
  14.3 3.9 %collective-permute-done.9.refs_2_ = f32[8,8,128]{2,1,0:T(8,128)S(1)} collective-permute-done((f32[8,8,128]{2,1,0:T(8,128)S(1)}, f32[8,8,128]{2,1,0:T(8,128)S(1)}, u32[]{:S(2)}, u32[]{:S(2)}) %collective-permute-start.9) | collective-permute-done | bytes 32800 | tf_op jit(solution)/shard_map/ppermute | solution.py:376
  18.2 2.8 %collective-permute-start.11 = (f32[16,8,128]{2,1,0:T(8,128)S(1)}, f32[16,8,128]{2,1,0:T(8,128)S(1)}, u32[]{:S(2)}, u32[]{:S(2)}) collective-permute-start(f32[16,8,128]{2,1,0:T(8,128)S(1)} %get-tuple-element.50), channel_id=1, source_target_pairs={{2,4},{4,2},{3,5},{5,3},{10,12},{12,10},{11,13},{13,11},{18,20},{2... | collective-permute-start | bytes 196616 | tf_op jit(solution)/shard_map/ppermute | solution.py:376
  21.1 2.1 %collective-permute-done.11.refs_4_ = f32[16,8,128]{2,1,0:T(8,128)S(1)} collective-permute-done((f32[16,8,128]{2,1,0:T(8,128)S(1)}, f32[16,8,128]{2,1,0:T(8,128)S(1)}, u32[]{:S(2)}, u32[]{:S(2)}) %collective-permute-start.11) | collective-permute-done | bytes 65568 | tf_op jit(solution)/shard_map/ppermute | solution.py:376
  23.4 1.8 %collective-permute-start.4 = (f32[264,128]{1,0:T(8,128)S(1)}, f32[264,128]{1,0:T(8,128)S(1)}, u32[]{:S(2)}, u32[]{:S(2)}) collective-permute-start(f32[264,128]{1,0:T(8,128)S(1)} %get-tuple-element.41), channel_id=1, source_target_pairs={{0,3},{1,2},{2,1},{3,0},{4,7},{5,6},{6,5},{7,4},{8,11},{9,10},{10,... | collective-permute-start | bytes 405512 | tf_op jit(solution)/shard_map/ppermute | solution.py:443
  25.8 0.7 %collective-permute-start.6 = (f32[264,128]{1,0:T(8,128)S(1)}, f32[264,128]{1,0:T(8,128)S(1)}, u32[]{:S(2)}, u32[]{:S(2)}) collective-permute-start(f32[264,128]{1,0:T(8,128)S(1)} %get-tuple-element.43), channel_id=1, source_target_pairs={{0,1},{1,0},{2,3},{3,2},{4,5},{5,4},{6,7},{7,6},{8,9},{9,8},{10,11... | collective-permute-start | bytes 405512 | tf_op jit(solution)/shard_map/ppermute | solution.py:443
  26.5 3.0 %shard_map.93 = (f32[16,64,128]{2,1,0:T(8,128)S(1)}, bf16[64,240]{1,0:T(8,128)(2,1)S(1)}, bf16[384,128]{1,0:T(8,128)(2,1)S(1)}, f32[24,128]{1,0:T(8,128)S(1)}) custom-call(f32[16,64,128]{2,1,0:T(8,128)S(1)} %get-tuple-element.45.own, f32[8,64,128]{2,1,0:T(8,128)S(1)} %collective-permute-done.7.refs_0_, f32[8,8,128]{2,1,0:T(8,128)S(1)} %collective-permute-done.8.refs_1_, ...), custom_call_target="tpu_custom_call" | custom-call | flops 4194304 | bytes 1048576 | tf_op jit(solution)/shard_map/pallas_call | solution.py:461
  29.5 1.9 %collective-permute-done.3.refs_4_ = f32[264,128]{1,0:T(8,128)S(1)} collective-permute-done((f32[264,128]{1,0:T(8,128)S(1)}, f32[264,128]{1,0:T(8,128)S(1)}, u32[]{:S(2)}, u32[]{:S(2)}) %collective-permute-start.3) | collective-permute-done | bytes 135200 | tf_op jit(solution)/shard_map/ppermute | solution.py:443
  32.5 1.1 %shard_map.94 = (f32[16,64,128]{2,1,0:T(8,128)S(1)}, f32[8,64,128]{2,1,0:T(8,128)S(1)}, f32[8,8,128]{2,1,0:T(8,128)S(1)}, f32[8,8,128]{2,1,0:T(8,128)S(1)}, f32[...) custom-call(f32[264,128]{1,0:T(8,128)S(1)} %get-tuple-element.36.refs_0_, f32[264,128]{1,0:T(8,128)S(1)} %collective-permute-done.refs_1_, ...), custom_call_target="tpu_custom_call" | custom-call | flops 4194304 | bytes 1048576 | tf_op jit(solution)/shard_map/pallas_call | solution.py:468
  34.2 1.7 %collective-permute-start.12 = (f32[16,8,128]{2,1,0:T(8,128)S(1)}, f32[16,8,128]{2,1,0:T(8,128)S(1)}, u32[]{:S(2)}, u32[]{:S(2)}) collective-permute-start(f32[16,8,128]{2,1,0:T(8,128)S(1)} %get-tuple-element.53), channel_id=1, source_target_pairs={{0,2},{2,0},{4,6},{6,4},{1,3},{3,1},{5,7},{7,5},{8,10},{10,8},{12,... | collective-permute-start | bytes 196616 | tf_op jit(solution)/shard_map/ppermute | solution.py:376
  35.9 2.1 %collective-permute-start.13 = (f32[16,8,128]{2,1,0:T(8,128)S(1)}, f32[16,8,128]{2,1,0:T(8,128)S(1)}, u32[]{:S(2)}, u32[]{:S(2)}) collective-permute-start(f32[16,8,128]{2,1,0:T(8,128)S(1)} %get-tuple-element.54), channel_id=1, source_target_pairs={{2,4},{4,2},{3,5},{5,3},{10,12},{12,10},{11,13},{13,11},{18,20},{2... | collective-permute-start | bytes 196616 | tf_op jit(solution)/shard_map/ppermute | solution.py:376
  38.6 2.4 %collective-permute-done.13.refs_1_ = f32[16,8,128]{2,1,0:T(8,128)S(1)} collective-permute-done((f32[16,8,128]{2,1,0:T(8,128)S(1)}, f32[16,8,128]{2,1,0:T(8,128)S(1)}, u32[]{:S(2)}, u32[]{:S(2)}) %collective-permute-start.13) | collective-permute-done | bytes 65568 | tf_op jit(solution)/shard_map/ppermute | solution.py:376
  40.9 1.0 %shard_map.95 = (f32[256,128]{1,0:T(8,128)S(1)}, f32[256,128]{1,0:T(8,128)S(1)}, f32[32,64,128]{2,1,0:T(8,128)S(1)}) custom-call(f32[16,64,128]{2,1,0:T(8,128)S(1)} %get-tuple-element.52.own, f32[16,8,128]{2,1,0:T(8,128)S(1)} %collective-permute-done.12.refs_0_, f32[16,8,128]{2,1,0:T(8,128)S(1)} %collective-permute-done.13.refs_1_, ...), custom_call_target="tpu_custom_call" | custom-call | flops 4194304 | bytes 1048576 | tf_op jit(solution)/shard_map/pallas_call | solution.py:473
  42.0 9.8 %collective-permute-start.14 = (f32[256,128]{1,0:T(8,128)S(1)}, f32[256,128]{1,0:T(8,128)S(1)}, u32[]{:S(2)}, u32[]{:S(2)}) collective-permute-start(f32[256,128]{1,0:T(8,128)S(1)} %get-tuple-element.59), channel_id=1, source_target_pairs={{0,8},{8,0},{16,24},{24,16},{1,9},{9,1},{17,25},{25,17},{2,10},{10... | collective-permute-start | bytes 393224 | tf_op jit(solution)/shard_map/ppermute | solution.py:350
  51.7 2.9 %collective-permute-start.17 = (f32[8,8,128]{2,1,0:T(8,128)S(1)}, f32[8,8,128]{2,1,0:T(8,128)S(1)}, u32[]{:S(2)}, u32[]{:S(2)}) collective-permute-start(f32[8,8,128]{2,1,0:T(8,128)S(1)} %get-tuple-element.63), channel_id=1, source_target_pairs={{2,5},{3,4},{4,3},{5,2},{10,13},{11,12},{12,11},{13,10},{18,21},{1... | collective-permute-start | bytes 98312 | tf_op jit(solution)/shard_map/ppermute | solution.py:376
  54.7 0.7 %collective-permute-done.16.refs_1_ = f32[8,8,128]{2,1,0:T(8,128)S(1)} collective-permute-done((f32[8,8,128]{2,1,0:T(8,128)S(1)}, f32[8,8,128]{2,1,0:T(8,128)S(1)}, u32[]{:S(2)}, u32[]{:S(2)}) %collective-permute-start.16) | collective-permute-done | bytes 32800 | tf_op jit(solution)/shard_map/ppermute | solution.py:376
  55.4 1.9 %collective-permute-done.17.refs_2_ = f32[8,8,128]{2,1,0:T(8,128)S(1)} collective-permute-done((f32[8,8,128]{2,1,0:T(8,128)S(1)}, f32[8,8,128]{2,1,0:T(8,128)S(1)}, u32[]{:S(2)}, u32[]{:S(2)}) %collective-permute-start.17) | collective-permute-done | bytes 32800 | tf_op jit(solution)/shard_map/ppermute | solution.py:376
  57.3 0.9 %shard_map.96 = (f32[256,128]{1,0:T(8,128)S(1)}, f32[256,128]{1,0:T(8,128)S(1)}) custom-call(f32[256,128]{1,0:T(8,128)S(1)} %mul.28.after, f32[32,64,128]{2,1,0:T(8,128)S(1)} %get-tuple-element.60.before, f32[8,64,128]{2,1,0:T(8,128)S(1)} %collective-permute-done.15.refs_0_, f32[8,8,128]{2,1,0:T(8,128)S(1)} %collective-permute-done.16.refs_1_, ...), custom_call_target="tpu_custom_call" | custom-call | flops 4194304 | bytes 1048576 | tf_op jit(solution)/shard_map/pallas_call | solution.py:489
  58.2 1.3 %collective-permute-start.18 = (f32[256,128]{1,0:T(8,128)S(1)}, f32[256,128]{1,0:T(8,128)S(1)}, u32[]{:S(2)}, u32[]{:S(2)}) collective-permute-start(f32[256,128]{1,0:T(8,128)S(1)} %get-tuple-element.65), channel_id=1, source_target_pairs={{0,8},{8,0},{16,24},{24,16},{1,9},{9,1},{17,25},{25,17},{2,10},{10... | collective-permute-start | bytes 393224 | tf_op jit(solution)/shard_map/ppermute | solution.py:350
  59.5 1.2 %collective-permute-start.20 = (f32[256,128]{1,0:T(8,128)S(1)}, f32[256,128]{1,0:T(8,128)S(1)}, u32[]{:S(2)}, u32[]{:S(2)}) collective-permute-start(f32[256,128]{1,0:T(8,128)S(1)} %mul.28.after), channel_id=1, source_target_pairs={{0,16},{8,24},{16,0},{24,8},{1,17},{9,25},{17,1},{25,9},{2,18},{10... | collective-permute-start | bytes 393224 | tf_op jit(solution)/shard_map/ppermute | solution.py:350
  60.8 1.0 %collective-permute-start.19 = (f32[256,128]{1,0:T(8,128)S(1)}, f32[256,128]{1,0:T(8,128)S(1)}, u32[]{:S(2)}, u32[]{:S(2)}) collective-permute-start(f32[256,128]{1,0:T(8,128)S(1)} %mul.29), channel_id=1, source_target_pairs={{0,16},{8,24},{16,0},{24,8},{1,17},{9,25},{17,1},{25,9},{2,18},{10... | collective-permute-start | bytes 393224 | tf_op jit(solution)/shard_map/ppermute | solution.py:350
  61.8 2.7 %collective-permute-done.20 = f32[256,128]{1,0:T(8,128)S(1)} collective-permute-done((f32[256,128]{1,0:T(8,128)S(1)}, f32[256,128]{1,0:T(8,128)S(1)}, u32[]{:S(2)}, u32[]{:S(2)}) %collective-permute-start.20) | collective-permute-done | bytes 131104 | tf_op jit(solution)/shard_map/ppermute | solution.py:350
  64.5 1.5 %collective-permute-start.22 = (f32[256,128]{1,0:T(8,128)S(1)}, f32[256,128]{1,0:T(8,128)S(1)}, u32[]{:S(2)}, u32[]{:S(2)}) collective-permute-start(f32[256,128]{1,0:T(8,128)S(1)} %bitcast_multiply_fusion.1), channel_id=1, source_target_pairs={{0,8},{8,0},{16,24},{24,16},{1,9},{9,1},{17,25},{25,17},{2,10},{10... | collective-permute-start | bytes 393224 | tf_op jit(solution)/shard_map/ppermute | solution.py:350
  66.1 1.2 %collective-permute-done.19 = f32[256,128]{1,0:T(8,128)S(1)} collective-permute-done((f32[256,128]{1,0:T(8,128)S(1)}, f32[256,128]{1,0:T(8,128)S(1)}, u32[]{:S(2)}, u32[]{:S(2)}) %collective-permute-start.19) | collective-permute-done | bytes 131104 | tf_op jit(solution)/shard_map/ppermute | solution.py:350
  67.3 1.0 %collective-permute-start.21 = (f32[256,128]{1,0:T(8,128)S(1)}, f32[256,128]{1,0:T(8,128)S(1)}, u32[]{:S(2)}, u32[]{:S(2)}) collective-permute-start(f32[256,128]{1,0:T(8,128)S(1)} %bitcast_multiply_fusion), channel_id=1, source_target_pairs={{0,8},{8,0},{16,24},{24,16},{1,9},{9,1},{17,25},{25,17},{2,10},{10... | collective-permute-start | bytes 393224 | tf_op jit(solution)/shard_map/ppermute | solution.py:350
  68.4 0.7 %shard_map.97.refs_1_ = f32[64,16,128]{2,1,0:T(8,128)} custom-call(f32[32,8,128]{2,1,0:T(8,128)S(1)} %bitcast.13, f32[32,8,128]{2,1,0:T(8,128)S(1)} %bitcast.15), custom_call_target="tpu_custom_call" | custom-call | flops 4194304 | bytes 1048576 | tf_op jit(solution)/shard_map/pallas_call | solution.py:346
  69.8 0.7 shard_map.99
  (35 shorter events, 4.2 us)
Async XLA Ops:
  0.0 1.9 %copy-start = (f32[64,16,128]{2,1,0:T(8,128)S(1)}, f32[64,16,128]{2,1,0:T(8,128)}, u32[]{:S(2)}) copy-start(f32[64,16,128]{2,1,0:T(8,128)} %param.9) | copy-start | bytes 1572868
  2.2 23.6 %collective-permute-start.7 = (f32[8,64,128]{2,1,0:T(8,128)S(1)}, f32[8,64,128]{2,1,0:T(8,128)S(1)}, u32[]{:S(2)}, u32[]{:S(2)}) collective-permute-start(f32[8,64,128]{2,1,0:T(8,128)S(1)} %get-tuple-element.46), channel_id=1, source_target_pairs={{0,1},{1,0},{2,3},{3,2},{4,5},{5,4},{6,7},{7,6},{8,9},{9,8},{10,11... | collective-permute-start | bytes 786440 | tf_op jit(solution)/shard_map/ppermute | solution.py:376
  3.5 19.9 %collective-permute-start = (f32[264,128]{1,0:T(8,128)S(1)}, f32[264,128]{1,0:T(8,128)S(1)}, u32[]{:S(2)}, u32[]{:S(2)}) collective-permute-start(f32[264,128]{1,0:T(8,128)S(1)} %get-tuple-element.37), channel_id=1, source_target_pairs={{0,7},{1,6},{2,5},{3,4},{4,3},{5,2},{6,1},{7,0},{8,15},{9,14},{10,... | collective-permute-start | bytes 405512 | tf_op jit(solution)/shard_map/ppermute | solution.py:443
  4.7 20.5 %collective-permute-start.1 = (f32[264,128]{1,0:T(8,128)S(1)}, f32[264,128]{1,0:T(8,128)S(1)}, u32[]{:S(2)}, u32[]{:S(2)}) collective-permute-start(f32[264,128]{1,0:T(8,128)S(1)} %get-tuple-element.38), channel_id=1, source_target_pairs={{0,6},{1,7},{2,4},{3,5},{4,2},{5,3},{6,0},{7,1},{8,14},{9,15},{10,... | collective-permute-start | bytes 405512 | tf_op jit(solution)/shard_map/ppermute | solution.py:443
  4.9 9.4 %collective-permute-start.8 = (f32[8,8,128]{2,1,0:T(8,128)S(1)}, f32[8,8,128]{2,1,0:T(8,128)S(1)}, u32[]{:S(2)}, u32[]{:S(2)}) collective-permute-start(f32[8,8,128]{2,1,0:T(8,128)S(1)} %get-tuple-element.47), channel_id=1, source_target_pairs={{0,3},{1,2},{2,1},{3,0},{4,7},{5,6},{6,5},{7,4},{8,11},{9,10},{10,... | collective-permute-start | bytes 98312 | tf_op jit(solution)/shard_map/ppermute | solution.py:376
  7.9 10.3 %collective-permute-start.9 = (f32[8,8,128]{2,1,0:T(8,128)S(1)}, f32[8,8,128]{2,1,0:T(8,128)S(1)}, u32[]{:S(2)}, u32[]{:S(2)}) collective-permute-start(f32[8,8,128]{2,1,0:T(8,128)S(1)} %get-tuple-element.48), channel_id=1, source_target_pairs={{2,5},{3,4},{4,3},{5,2},{10,13},{11,12},{12,11},{13,10},{18,21},{1... | collective-permute-start | bytes 98312 | tf_op jit(solution)/shard_map/ppermute | solution.py:376
  14.3 6.6 %collective-permute-start.10 = (f32[16,8,128]{2,1,0:T(8,128)S(1)}, f32[16,8,128]{2,1,0:T(8,128)S(1)}, u32[]{:S(2)}, u32[]{:S(2)}) collective-permute-start(f32[16,8,128]{2,1,0:T(8,128)S(1)} %get-tuple-element.49), channel_id=1, source_target_pairs={{0,2},{2,0},{4,6},{6,4},{1,3},{3,1},{5,7},{7,5},{8,10},{10,8},{12,... | collective-permute-start | bytes 196616 | tf_op jit(solution)/shard_map/ppermute | solution.py:376
  18.2 5.0 %collective-permute-start.11 = (f32[16,8,128]{2,1,0:T(8,128)S(1)}, f32[16,8,128]{2,1,0:T(8,128)S(1)}, u32[]{:S(2)}, u32[]{:S(2)}) collective-permute-start(f32[16,8,128]{2,1,0:T(8,128)S(1)} %get-tuple-element.50), channel_id=1, source_target_pairs={{2,4},{4,2},{3,5},{5,3},{10,12},{12,10},{11,13},{13,11},{18,20},{2... | collective-permute-start | bytes 196616 | tf_op jit(solution)/shard_map/ppermute | solution.py:376
  21.0 8.6 %collective-permute-start.2 = (f32[264,128]{1,0:T(8,128)S(1)}, f32[264,128]{1,0:T(8,128)S(1)}, u32[]{:S(2)}, u32[]{:S(2)}) collective-permute-start(f32[264,128]{1,0:T(8,128)S(1)} %get-tuple-element.39), channel_id=1, source_target_pairs={{0,5},{1,4},{2,7},{3,6},{4,1},{5,0},{6,3},{7,2},{8,13},{9,12},{10,... | collective-permute-start | bytes 405512 | tf_op jit(solution)/shard_map/ppermute | solution.py:443
  23.2 8.3 %collective-permute-start.3 = (f32[264,128]{1,0:T(8,128)S(1)}, f32[264,128]{1,0:T(8,128)S(1)}, u32[]{:S(2)}, u32[]{:S(2)}) collective-permute-start(f32[264,128]{1,0:T(8,128)S(1)} %get-tuple-element.40), channel_id=1, source_target_pairs={{0,4},{1,5},{2,6},{3,7},{4,0},{5,1},{6,2},{7,3},{8,12},{9,13},{10,... | collective-permute-start | bytes 405512 | tf_op jit(solution)/shard_map/ppermute | solution.py:443
  23.4 8.1 %collective-permute-start.4 = (f32[264,128]{1,0:T(8,128)S(1)}, f32[264,128]{1,0:T(8,128)S(1)}, u32[]{:S(2)}, u32[]{:S(2)}) collective-permute-start(f32[264,128]{1,0:T(8,128)S(1)} %get-tuple-element.41), channel_id=1, source_target_pairs={{0,3},{1,2},{2,1},{3,0},{4,7},{5,6},{6,5},{7,4},{8,11},{9,10},{10,... | collective-permute-start | bytes 405512 | tf_op jit(solution)/shard_map/ppermute | solution.py:443
  25.2 7.0 %collective-permute-start.5 = (f32[264,128]{1,0:T(8,128)S(1)}, f32[264,128]{1,0:T(8,128)S(1)}, u32[]{:S(2)}, u32[]{:S(2)}) collective-permute-start(f32[264,128]{1,0:T(8,128)S(1)} %get-tuple-element.42), channel_id=1, source_target_pairs={{0,2},{1,3},{2,0},{3,1},{4,6},{5,7},{6,4},{7,5},{8,10},{9,11},{10,... | collective-permute-start | bytes 405512 | tf_op jit(solution)/shard_map/ppermute | solution.py:443
  25.8 0.8 %copy-start.1 = (f32[1,17]{1,0:T(1,128)S(1)}, f32[1,17]{1,0:T(1,128)}, u32[]{:S(2)}) copy-start(f32[1,17]{1,0:T(1,128)} %refs_5_.1) | copy-start | bytes 208
  25.8 0.8 %copy-start.2 = (f32[1,17]{1,0:T(1,128)S(1)}, f32[1,17]{1,0:T(1,128)}, u32[]{:S(2)}) copy-start(f32[1,17]{1,0:T(1,128)} %refs_6_.1) | copy-start | bytes 208
  25.8 0.8 %copy-start.3 = (f32[1,33]{1,0:T(1,128)S(1)}, f32[1,33]{1,0:T(1,128)}, u32[]{:S(2)}) copy-start(f32[1,33]{1,0:T(1,128)} %refs_7_.1) | copy-start | bytes 400
  25.8 6.7 %collective-permute-start.6 = (f32[264,128]{1,0:T(8,128)S(1)}, f32[264,128]{1,0:T(8,128)S(1)}, u32[]{:S(2)}, u32[]{:S(2)}) collective-permute-start(f32[264,128]{1,0:T(8,128)S(1)} %get-tuple-element.43), channel_id=1, source_target_pairs={{0,1},{1,0},{2,3},{3,2},{4,5},{5,4},{6,7},{7,6},{8,9},{9,8},{10,11... | collective-permute-start | bytes 405512 | tf_op jit(solution)/shard_map/ppermute | solution.py:443
  33.6 23.7 %collective-permute-start.15 = (f32[8,64,128]{2,1,0:T(8,128)S(1)}, f32[8,64,128]{2,1,0:T(8,128)S(1)}, u32[]{:S(2)}, u32[]{:S(2)}) collective-permute-start(f32[8,64,128]{2,1,0:T(8,128)S(1)} %get-tuple-element.61), channel_id=1, source_target_pairs={{0,1},{1,0},{2,3},{3,2},{4,5},{5,4},{6,7},{7,6},{8,9},{9,8},{10,11... | collective-permute-start | bytes 786440 | tf_op jit(solution)/shard_map/ppermute | solution.py:376
  34.2 4.4 %collective-permute-start.12 = (f32[16,8,128]{2,1,0:T(8,128)S(1)}, f32[16,8,128]{2,1,0:T(8,128)S(1)}, u32[]{:S(2)}, u32[]{:S(2)}) collective-permute-start(f32[16,8,128]{2,1,0:T(8,128)S(1)} %get-tuple-element.53), channel_id=1, source_target_pairs={{0,2},{2,0},{4,6},{6,4},{1,3},{3,1},{5,7},{7,5},{8,10},{10,8},{12,... | collective-permute-start | bytes 196616 | tf_op jit(solution)/shard_map/ppermute | solution.py:376
  35.9 5.0 %collective-permute-start.13 = (f32[16,8,128]{2,1,0:T(8,128)S(1)}, f32[16,8,128]{2,1,0:T(8,128)S(1)}, u32[]{:S(2)}, u32[]{:S(2)}) collective-permute-start(f32[16,8,128]{2,1,0:T(8,128)S(1)} %get-tuple-element.54), channel_id=1, source_target_pairs={{2,4},{4,2},{3,5},{5,3},{10,12},{12,10},{11,13},{13,11},{18,20},{2... | collective-permute-start | bytes 196616 | tf_op jit(solution)/shard_map/ppermute | solution.py:376
  42.0 12.7 %collective-permute-start.14 = (f32[256,128]{1,0:T(8,128)S(1)}, f32[256,128]{1,0:T(8,128)S(1)}, u32[]{:S(2)}, u32[]{:S(2)}) collective-permute-start(f32[256,128]{1,0:T(8,128)S(1)} %get-tuple-element.59), channel_id=1, source_target_pairs={{0,8},{8,0},{16,24},{24,16},{1,9},{9,1},{17,25},{25,17},{2,10},{10... | collective-permute-start | bytes 393224 | tf_op jit(solution)/shard_map/ppermute | solution.py:350
  51.7 3.7 %collective-permute-start.16 = (f32[8,8,128]{2,1,0:T(8,128)S(1)}, f32[8,8,128]{2,1,0:T(8,128)S(1)}, u32[]{:S(2)}, u32[]{:S(2)}) collective-permute-start(f32[8,8,128]{2,1,0:T(8,128)S(1)} %get-tuple-element.62), channel_id=1, source_target_pairs={{0,3},{1,2},{2,1},{3,0},{4,7},{5,6},{6,5},{7,4},{8,11},{9,10},{10,... | collective-permute-start | bytes 98312 | tf_op jit(solution)/shard_map/ppermute | solution.py:376
  51.7 5.5 %collective-permute-start.17 = (f32[8,8,128]{2,1,0:T(8,128)S(1)}, f32[8,8,128]{2,1,0:T(8,128)S(1)}, u32[]{:S(2)}, u32[]{:S(2)}) collective-permute-start(f32[8,8,128]{2,1,0:T(8,128)S(1)} %get-tuple-element.63), channel_id=1, source_target_pairs={{2,5},{3,4},{4,3},{5,2},{10,13},{11,12},{12,11},{13,10},{18,21},{1... | collective-permute-start | bytes 98312 | tf_op jit(solution)/shard_map/ppermute | solution.py:376
  58.2 2.5 %collective-permute-start.18 = (f32[256,128]{1,0:T(8,128)S(1)}, f32[256,128]{1,0:T(8,128)S(1)}, u32[]{:S(2)}, u32[]{:S(2)}) collective-permute-start(f32[256,128]{1,0:T(8,128)S(1)} %get-tuple-element.65), channel_id=1, source_target_pairs={{0,8},{8,0},{16,24},{24,16},{1,9},{9,1},{17,25},{25,17},{2,10},{10... | collective-permute-start | bytes 393224 | tf_op jit(solution)/shard_map/ppermute | solution.py:350
  59.5 5.0 %collective-permute-start.20 = (f32[256,128]{1,0:T(8,128)S(1)}, f32[256,128]{1,0:T(8,128)S(1)}, u32[]{:S(2)}, u32[]{:S(2)}) collective-permute-start(f32[256,128]{1,0:T(8,128)S(1)} %mul.28.after), channel_id=1, source_target_pairs={{0,16},{8,24},{16,0},{24,8},{1,17},{9,25},{17,1},{25,9},{2,18},{10... | collective-permute-start | bytes 393224 | tf_op jit(solution)/shard_map/ppermute | solution.py:350
  60.8 6.6 %collective-permute-start.19 = (f32[256,128]{1,0:T(8,128)S(1)}, f32[256,128]{1,0:T(8,128)S(1)}, u32[]{:S(2)}, u32[]{:S(2)}) collective-permute-start(f32[256,128]{1,0:T(8,128)S(1)} %mul.29), channel_id=1, source_target_pairs={{0,16},{8,24},{16,0},{24,8},{1,17},{9,25},{17,1},{25,9},{2,18},{10... | collective-permute-start | bytes 393224 | tf_op jit(solution)/shard_map/ppermute | solution.py:350
  64.5 3.8 %collective-permute-start.22 = (f32[256,128]{1,0:T(8,128)S(1)}, f32[256,128]{1,0:T(8,128)S(1)}, u32[]{:S(2)}, u32[]{:S(2)}) collective-permute-start(f32[256,128]{1,0:T(8,128)S(1)} %bitcast_multiply_fusion.1), channel_id=1, source_target_pairs={{0,8},{8,0},{16,24},{24,16},{1,9},{9,1},{17,25},{25,17},{2,10},{10... | collective-permute-start | bytes 393224 | tf_op jit(solution)/shard_map/ppermute | solution.py:350
  67.3 2.4 %collective-permute-start.21 = (f32[256,128]{1,0:T(8,128)S(1)}, f32[256,128]{1,0:T(8,128)S(1)}, u32[]{:S(2)}, u32[]{:S(2)}) collective-permute-start(f32[256,128]{1,0:T(8,128)S(1)} %bitcast_multiply_fusion), channel_id=1, source_target_pairs={{0,8},{8,0},{16,24},{24,16},{1,9},{9,1},{17,25},{25,17},{2,10},{10... | collective-permute-start | bytes 393224 | tf_op jit(solution)/shard_map/ppermute | solution.py:350
where the time goes:
time: 70.7 us; the launch traced here: 70.5 us
  starting transfers between devices  39.2 us (55%)
  waiting for transfers between devices  20.7 us (29%)
  Pallas kernels  10.3 us (15%)
    ppermute x10, starting transfers between devices, halo(): lax.ppermute(edge, axis, moves)  18.6 us
    ppermute x6, starting transfers between devices, swap(): lax.ppermute(x, axis, [(i, i ^ mask) for i in range(lax.axis_size(axis))])  15.9 us
    ppermute x10, waiting for transfers between devices, halo(): lax.ppermute(edge, axis, moves)  13.7 us
    ppermute x7, starting transfers between devices, local(): chunks.append(lax.ppermute(packed[s], ('bx', 'by'), pair))  4.81 us
    ppermute x6, waiting for transfers between devices, swap(): lax.ppermute(x, axis, [(i, i ^ mask) for i in range(lax.axis_size(axis))])  3.96 us
    pallas_call x1, Pallas kernels, local(): call(blur_kernel, shapes, work, specs, limit=BLUR_LIMIT)  2.98 us
    ppermute x7, waiting for transfers between devices, local(): chunks.append(lax.ppermute(packed[s], ('bx', 'by'), pair))  2.97 us
    pallas_call x3, Pallas kernels, store(): return call(kernel, [(CX, CY, CZ)], sems, specs, [ANY], aliases)(*values)[0]  2.08 us
  transfers between devices with their start and end apart: 23, of which 12 were waited for; matrix products, arithmetic and copies ran while one was open for 0% of the time, Pallas kernels for 8%

commit v1 on v0

--- a/solution.py
+++ b/solution.py
@@ -134,16 +134,19 @@
 
 def put_edges(volume, outs):
     odd_x, odd_y = sides()
-    at_x = [pl.multiple_of((1 - odd_x) * (CX - R), R), pl.multiple_of(odd_x * (CX - R), R)]
-    at_y = [(1 - odd_y) * (CY - R), odd_y * (CY - R)]
-    for phase in range((len(outs) - 2) // 3):
-        whole, first, second = outs[3 * phase : 3 * phase + 3]
-        rows = pl.ds(at_y[phase], R)
-        whole[...] = volume[rows]
-        first[...] = volume[rows, pl.ds(at_x[0], R), :]
-        second[...] = volume[rows, pl.ds(at_x[1], R), :]
-    outs[-2][...] = volume[:, pl.ds(at_x[0], R), :]
-    outs[-1][...] = volume[:, pl.ds(at_x[1], R), :]
+    for phase, out in enumerate(outs[:-2]):
+        out[...] = volume[pl.ds((odd_y if phase else 1 - odd_y) * (CY - R), R)]
+    for phase, out in enumerate(outs[-2:]):
+        at = (odd_x if phase else 1 - odd_x) * (CX - R)
+        out[...] = volume[:, pl.ds(pl.multiple_of(at, R), R), :]
+
+
+def corner_kernel(xa, xb, *outs):
+    _, odd_y = sides()
+    for phase, out in enumerate(outs):
+        rows = pl.ds((odd_y if phase else 1 - odd_y) * (CY - R), R)
+        out[0] = xa[rows]
+        out[1] = xb[rows]
 
 
 def turn_kernel(estimate, after, turned, *edges):
@@ -224,21 +227,21 @@
     padded[:count, pl.ds(pl.multiple_of(odd_x * (CX + R), R), R), :] = xb[...]
 
 
-def far_lines(own, x_halos, y_halos, band_x, padded, lines):
+def far_lines(own, x_halos, y_halo, band_x, padded, lines):
     _, odd_y = sides()
     put_x(own, *x_halos, padded, CY)
     smear_x(padded, CY, band_x, lines, R)
     far = (CY + R) * odd_y
-    if y_halos:
-        put_x(*y_halos, padded, R)
+    if y_halo:
+        put_x(y_halo[0], y_halo[1].at[0], y_halo[1].at[1], padded, R)
         smear_x(padded, R, band_x, lines, far)
     else:
         lines[pl.ds(far, R)] = jnp.zeros((R, CX, CZ), F32)
 
 
-def near_lines(y_halos, band_x, padded, lines):
+def near_lines(y_halo, band_x, padded, lines):
     _, odd_y = sides()
-    put_x(*y_halos, padded, R)
+    put_x(y_halo[0], y_halo[1].at[0], y_halo[1].at[1], padded, R)
     smear_x(padded, R, band_x, lines, (CY + R) * (1 - odd_y))
 
 
@@ -246,8 +249,8 @@
     halos, (kx, ky, kz, out, *bands) = refs[:-13], refs[-13:]
     band_x, band_z, taps, padded, lines, held = bands[3:]
     make_bands(kx, ky, kz, *bands[3:6], *bands[:3])
-    far_lines(own, halos[-2:], halos[3:-2], band_x, padded, lines)
-    near_lines(halos[:3], band_x, padded, lines)
+    far_lines(own, halos[-2:], halos[2:-2], band_x, padded, lines)
+    near_lines(halos[:2], band_x, padded, lines)
     for start in range(0, CY, HY):
         for y, value in enumerate(smear_yz(lines, start, taps, band_z, held)):
             out[start + y] = value
@@ -272,7 +275,7 @@
 
 
 def near_kernel(after, before, *refs):
-    halos, (band_x, band_z, taps, mine, other, padded, held, whole, lines) = refs[:3], refs[3:]
+    halos, (band_x, band_z, taps, mine, other, padded, held, whole, lines) = refs[:2], refs[2:]
     _, odd_y = sides()
     lines[R : R + CY] = before[R : R + CY]
     near_lines(halos, band_x, padded, lines)
@@ -358,23 +361,18 @@
     return [first] + ([second] if second else [])
 
 
-def halo_pairs():
-    x_pairs, y_pairs, wide = pairs("bx"), pairs("by"), lax.axis_size("by")
+def halo(edges):
+    x_pairs, y_pairs = pairs("bx"), pairs("by")
     x_pairs = x_pairs + [[]] * (2 - len(x_pairs))
-    out = []
-    for ys in y_pairs:
-        out.append(("by", ys))
-        for xs in x_pairs:
-            moves = [(a * wide + c, b * wide + d) for a, b in xs for c, d in ys]
-            out.append((("bx", "by"), moves))
-    return out + [("bx", xs) for xs in x_pairs]
-
-
-def halo(edges):
-    got = []
-    for edge, (axis, moves) in zip(edges, halo_pairs()):
-        got.append(lax.ppermute(edge, axis, moves) if moves else jnp.zeros_like(edge))
-    return got
+
+    def move(value, axis, moves):
+        return lax.ppermute(value, axis, moves) if moves else jnp.zeros_like(value)
+
+    got_y = [move(e, "by", p) for e, p in zip(edges, y_pairs)]
+    got_x = [move(e, "bx", p) for e, p in zip(edges[-2:], x_pairs)]
+    cut = call(corner_kernel, [(2, R, R, CZ)] * len(y_pairs), in_specs=[VM] * 2)(*got_x)
+    got_c = [move(e, "by", p) for e, p in zip(cut, y_pairs)]
+    return [value for both in zip(got_y, got_c) for value in both] + got_x
 
 
 def generic_exchange(bricks, observed, target, slot, count, weight):
@@ -415,7 +413,7 @@
     bricks = count_bx * count_by
     phases = len(pairs("by"))
     flat = estimate.reshape(CX * CY, CZ)
-    edge_shapes = [(R, CX, CZ), (R, R, CZ), (R, R, CZ)] * phases + [(CY, R, CZ)] * 2
+    edge_shapes = [(R, CX, CZ)] * phases + [(CY, R, CZ)] * 2
     brick, quarter, lines = (CY, CX, CZ), (HX * HY, CZ), (CY + 2 * R, CX, CZ)
     padded, held = pltpu.VMEM((CY, XE, CZ), F32), pltpu.VMEM((HY, CX, CZ), F32)
     whole = pltpu.VMEM((CX * HY, CZ), F32)
@@ -469,9 +467,12 @@
         *chunks, blurred
     )
     around = halo(edges)
-    near_halos, far_halos = around[:3], around[3:]
+    near_halos, far_halos = around[:2], around[2:]
     mine, other, before = call(
-        far_kernel, [quarter, quarter, lines], [padded, held, whole], [VM] * (len(far_halos) + 4)
+        far_kernel,
+        [quarter, quarter, lines],
+        [padded, held, whole],
+        [VM] * (len(far_halos) + 4),
     )(ratio, *far_halos, *bands)
     core, odd_y = lax.axis_index("view") % 2, lax.axis_index("by") % 2
 
@@ -486,7 +487,7 @@
 
     mine = paired(mine, other)
     work = [padded, held, whole, pltpu.VMEM(lines, F32)]
-    near = call(near_kernel, [quarter, quarter], work, [ANY] + [VM] * 7)(
+    near = call(near_kernel, [quarter, quarter], work, [ANY] + [VM] * 6)(
         mine, before, *near_halos, *bands
     )
     far_mine, far_other = product(mine, odd_y, estimate)

time: 70.7 us -> 63.3 us (0.90)
  the two profiles are of different devices: /device:TPU:9 before, /device:TPU:13 now
where the time goes in v1:
time: 63.3 us; the launch traced here: 63.1 us
  starting transfers between devices  29 us (46%)
  waiting for transfers between devices  23.6 us (37%)
  Pallas kernels  10.3 us (16%)
    ppermute x8, waiting for transfers between devices, move(): return lax.ppermute(value, axis, moves) if moves else jnp.zeros_like(value)  14.8 us
    ppermute x6, starting transfers between devices, swap(): lax.ppermute(x, axis, [(i, i ^ mask) for i in range(lax.axis_size(axis))])  11.7 us
    ppermute x8, starting transfers between devices, move(): return lax.ppermute(value, axis, moves) if moves else jnp.zeros_like(value)  11.1 us
    ppermute x7, starting transfers between devices, local(): chunks.append(lax.ppermute(packed[s], ('bx', 'by'), pair))  6.11 us
    ppermute x6, waiting for transfers between devices, swap(): lax.ppermute(x, axis, [(i, i ^ mask) for i in range(lax.axis_size(axis))])  4.94 us
    ppermute x7, waiting for transfers between devices, local(): chunks.append(lax.ppermute(packed[s], ('bx', 'by'), pair))  3.9 us
    pallas_call x1, Pallas kernels, local(): call(blur_kernel, shapes, work, specs, limit=BLUR_LIMIT)  2.97 us
    pallas_call x3, Pallas kernels, store(): return call(kernel, [(CX, CY, CZ)], sems, specs, [ANY], aliases)(*values)[0]  2.08 us
  transfers between devices with their start and end apart: 21, of which 11 were waited for; matrix products, arithmetic and copies ran while one was open for 0% of the time, Pallas kernels for 9%

profile of v1, /device:TPU:13, one launch (start us, length us, event | category | flops | bytes accessed | tf_op | source)
XLA Modules:
  0.0 63.1 jit_solution(1367400706539993901)
XLA Ops:
  0.0 1.9 %shard_map.91 = (f32[264,128]{1,0:T(8,128)S(1)}, f32[264,128]{1,0:T(8,128)S(1)}, f32[264,128]{1,0:T(8,128)S(1)}, f32[264,128]{1,0:T(8,128)S(1)}, f32[264,128]{1,...) custom-call(f32[256,512]{1,0:T(8,128)} %bitcast.16, ...), custom_call_target="tpu_custom_call" | custom-call | flops 4194304 | bytes 1048576 | tf_op jit(solution)/shard_map/pallas_call | solution.py:426
  2.5 2.3 %collective-permute-start = (f32[264,128]{1,0:T(8,128)S(1)}, f32[264,128]{1,0:T(8,128)S(1)}, u32[]{:S(2)}, u32[]{:S(2)}) collective-permute-start(f32[264,128]{1,0:T(8,128)S(1)} %get-tuple-element.33), channel_id=1, source_target_pairs={{0,7},{1,6},{2,5},{3,4},{4,3},{5,2},{6,1},{7,0},{8,15},{9,14},{10,... | collective-permute-start | bytes 405512 | tf_op jit(solution)/shard_map/ppermute | solution.py:441
  4.9 2.0 %collective-permute-start.8 = (f32[16,8,128]{2,1,0:T(8,128)S(1)}, f32[16,8,128]{2,1,0:T(8,128)S(1)}, u32[]{:S(2)}, u32[]{:S(2)}) collective-permute-start(f32[16,8,128]{2,1,0:T(8,128)S(1)} %get-tuple-element.43), channel_id=1, source_target_pairs={{0,2},{2,0},{4,6},{6,4},{1,3},{3,1},{5,7},{7,5},{8,10},{10,8},{12,... | collective-permute-start | bytes 196616 | tf_op jit(solution)/shard_map/ppermute | solution.py:369
  6.9 4.3 %collective-permute-start.9 = (f32[16,8,128]{2,1,0:T(8,128)S(1)}, f32[16,8,128]{2,1,0:T(8,128)S(1)}, u32[]{:S(2)}, u32[]{:S(2)}) collective-permute-start(f32[16,8,128]{2,1,0:T(8,128)S(1)} %get-tuple-element.44), channel_id=1, source_target_pairs={{2,4},{4,2},{3,5},{5,3},{10,12},{12,10},{11,13},{13,11},{18,20},{2... | collective-permute-start | bytes 196616 | tf_op jit(solution)/shard_map/ppermute | solution.py:369
  11.2 2.9 %collective-permute-done.8.xa.refs_2_ = f32[16,8,128]{2,1,0:T(8,128)S(1)} collective-permute-done((f32[16,8,128]{2,1,0:T(8,128)S(1)}, f32[16,8,128]{2,1,0:T(8,128)S(1)}, u32[]{:S(2)}, u32[]{:S(2)}) %collective-permute-start.8) | collective-permute-done | bytes 65568 | tf_op jit(solution)/shard_map/ppermute | solution.py:369
  14.1 4.1 %collective-permute-done.9.xb.refs_3_ = f32[16,8,128]{2,1,0:T(8,128)S(1)} collective-permute-done((f32[16,8,128]{2,1,0:T(8,128)S(1)}, f32[16,8,128]{2,1,0:T(8,128)S(1)}, u32[]{:S(2)}, u32[]{:S(2)}) %collective-permute-start.9) | collective-permute-done | bytes 65568 | tf_op jit(solution)/shard_map/ppermute | solution.py:369
  18.7 2.6 %collective-permute-done.10.refs_1_ = f32[2,8,8,128]{3,2,1,0:T(8,128)S(1)} collective-permute-done((f32[2,8,8,128]{3,2,1,0:T(8,128)S(1)}, f32[2,8,8,128]{3,2,1,0:T(8,128)S(1)}, u32[]{:S(2)}, u32[]{:S(2)}) %collective-permute-start.10) | collective-permute-done | bytes 65568 | tf_op jit(solution)/shard_map/ppermute | solution.py:369
  21.3 0.4 collective-permute-start.3
  21.8 1.6 %collective-permute-start.4 = (f32[264,128]{1,0:T(8,128)S(1)}, f32[264,128]{1,0:T(8,128)S(1)}, u32[]{:S(2)}, u32[]{:S(2)}) collective-permute-start(f32[264,128]{1,0:T(8,128)S(1)} %get-tuple-element.37), channel_id=1, source_target_pairs={{0,3},{1,2},{2,1},{3,0},{4,7},{5,6},{6,5},{7,4},{8,11},{9,10},{10,... | collective-permute-start | bytes 405512 | tf_op jit(solution)/shard_map/ppermute | solution.py:441
  23.5 1.2 %collective-permute-start.6 = (f32[264,128]{1,0:T(8,128)S(1)}, f32[264,128]{1,0:T(8,128)S(1)}, u32[]{:S(2)}, u32[]{:S(2)}) collective-permute-start(f32[264,128]{1,0:T(8,128)S(1)} %get-tuple-element.39), channel_id=1, source_target_pairs={{0,1},{1,0},{2,3},{3,2},{4,5},{5,4},{6,7},{7,6},{8,9},{9,8},{10,11... | collective-permute-start | bytes 405512 | tf_op jit(solution)/shard_map/ppermute | solution.py:441
  24.7 3.0 %shard_map.94 = (f32[16,64,128]{2,1,0:T(8,128)S(1)}, bf16[64,240]{1,0:T(8,128)(2,1)S(1)}, bf16[384,128]{1,0:T(8,128)(2,1)S(1)}, f32[24,128]{1,0:T(8,128)S(1)}) custom-call(f32[16,64,128]{2,1,0:T(8,128)S(1)} %get-tuple-element.41.own, f32[8,64,128]{2,1,0:T(8,128)S(1)} %collective-permute-done.7.refs_0_, f32[2,8,8,128]{3,2,1,0:T(8,128)S(1)} %collective-permute-done.10.refs_1_, ...), custom_call_target="tpu_custom_call" | custom-call | flops 4194304 | bytes 1048576 | tf_op jit(solution)/shard_map/pallas_call | solution.py:459
  27.7 1.7 %collective-permute-done.3.refs_4_ = f32[264,128]{1,0:T(8,128)S(1)} collective-permute-done((f32[264,128]{1,0:T(8,128)S(1)}, f32[264,128]{1,0:T(8,128)S(1)}, u32[]{:S(2)}, u32[]{:S(2)}) %collective-permute-start.3) | collective-permute-done | bytes 135200 | tf_op jit(solution)/shard_map/ppermute | solution.py:441
  29.6 2.0 %collective-permute-done.5.refs_6_ = f32[264,128]{1,0:T(8,128)S(1)} collective-permute-done((f32[264,128]{1,0:T(8,128)S(1)}, f32[264,128]{1,0:T(8,128)S(1)}, u32[]{:S(2)}, u32[]{:S(2)}) %collective-permute-start.5) | collective-permute-done | bytes 135200 | tf_op jit(solution)/shard_map/ppermute | solution.py:441
  31.6 1.1 %shard_map.95 = (f32[16,64,128]{2,1,0:T(8,128)S(1)}, f32[8,64,128]{2,1,0:T(8,128)S(1)}, f32[16,8,128]{2,1,0:T(8,128)S(1)}, f32[16,8,128]{2,1,0:T(8,128)S(1)}) custom-call(f32[264,128]{1,0:T(8,128)S(1)} %get-tuple-element.32.refs_0_, f32[264,128]{1,0:T(8,128)S(1)} %collective-permute-done.refs_1_, f32[264,128]{1,0:T(8,128)S(1)} %collective-permute-done.1.refs_2_, ...), custom_call_target="tpu_custom_call" | custom-call | flops 4194304 | bytes 1048576 | tf_op jit(solution)/shard_map/pallas_call | solution.py:466
  32.7 1.2 %collective-permute-start.14 = (f32[8,64,128]{2,1,0:T(8,128)S(1)}, f32[8,64,128]{2,1,0:T(8,128)S(1)}, u32[]{:S(2)}, u32[]{:S(2)}) collective-permute-start(f32[8,64,128]{2,1,0:T(8,128)S(1)} %get-tuple-element.55), channel_id=1, source_target_pairs={{0,1},{1,0},{2,3},{3,2},{4,5},{5,4},{6,7},{7,6},{8,9},{9,8},{10,11... | collective-permute-start | bytes 786440 | tf_op jit(solution)/shard_map/ppermute | solution.py:369
  34.3 2.8 %collective-permute-start.12 = (f32[16,8,128]{2,1,0:T(8,128)S(1)}, f32[16,8,128]{2,1,0:T(8,128)S(1)}, u32[]{:S(2)}, u32[]{:S(2)}) collective-permute-start(f32[16,8,128]{2,1,0:T(8,128)S(1)} %get-tuple-element.48), channel_id=1, source_target_pairs={{2,4},{4,2},{3,5},{5,3},{10,12},{12,10},{11,13},{13,11},{18,20},{2... | collective-permute-start | bytes 196616 | tf_op jit(solution)/shard_map/ppermute | solution.py:369
  37.1 2.5 %collective-permute-done.12.refs_1_.xb = f32[16,8,128]{2,1,0:T(8,128)S(1)} collective-permute-done((f32[16,8,128]{2,1,0:T(8,128)S(1)}, f32[16,8,128]{2,1,0:T(8,128)S(1)}, u32[]{:S(2)}, u32[]{:S(2)}) %collective-permute-start.12) | collective-permute-done | bytes 65568 | tf_op jit(solution)/shard_map/ppermute | solution.py:369
  39.6 1.0 %shard_map.96 = (f32[256,128]{1,0:T(8,128)S(1)}, f32[256,128]{1,0:T(8,128)S(1)}, f32[32,64,128]{2,1,0:T(8,128)S(1)}) custom-call(f32[16,64,128]{2,1,0:T(8,128)S(1)} %get-tuple-element.46.own, f32[16,8,128]{2,1,0:T(8,128)S(1)} %collective-permute-done.11.refs_0_.xa, f32[16,8,128]{2,1,0:T(8,128)S(1)} %collective-permute-done.12.refs_1_.xb, ...), custom_call_target="tpu_custom_call" | custom-call | flops 4194304 | bytes 1048576 | tf_op jit(solution)/shard_map/pallas_call | solution.py:471
  40.7 6.0 %collective-permute-start.13 = (f32[256,128]{1,0:T(8,128)S(1)}, f32[256,128]{1,0:T(8,128)S(1)}, u32[]{:S(2)}, u32[]{:S(2)}) collective-permute-start(f32[256,128]{1,0:T(8,128)S(1)} %get-tuple-element.53), channel_id=1, source_target_pairs={{0,8},{8,0},{16,24},{24,16},{1,9},{9,1},{17,25},{25,17},{2,10},{10... | collective-permute-start | bytes 393224 | tf_op jit(solution)/shard_map/ppermute | solution.py:353
  46.6 1.0 %collective-permute-done.13 = f32[256,128]{1,0:T(8,128)S(1)} collective-permute-done((f32[256,128]{1,0:T(8,128)S(1)}, f32[256,128]{1,0:T(8,128)S(1)}, u32[]{:S(2)}, u32[]{:S(2)}) %collective-permute-start.13) | collective-permute-done | bytes 131104 | tf_op jit(solution)/shard_map/ppermute | solution.py:353
  47.6 2.6 %collective-permute-done.15.refs_1_ = f32[2,8,8,128]{3,2,1,0:T(8,128)S(1)} collective-permute-done((f32[2,8,8,128]{3,2,1,0:T(8,128)S(1)}, f32[2,8,8,128]{3,2,1,0:T(8,128)S(1)}, u32[]{:S(2)}, u32[]{:S(2)}) %collective-permute-start.15) | collective-permute-done | bytes 65568 | tf_op jit(solution)/shard_map/ppermute | solution.py:369
  50.2 0.9 %shard_map.98 = (f32[256,128]{1,0:T(8,128)S(1)}, f32[256,128]{1,0:T(8,128)S(1)}) custom-call(f32[256,128]{1,0:T(8,128)S(1)} %mul.28.after, f32[32,64,128]{2,1,0:T(8,128)S(1)} %get-tuple-element.54.before, f32[8,64,128]{2,1,0:T(8,128)S(1)} %collective-permute-done.14.refs_0_, f32[2,8,8,128]{3,2,1,0:T(8,128)S(1)} %collective-permute-done.15.refs_1_, ...), custom_call_target="tpu_custom_call" | custom-call | flops 4194304 | bytes 1048576 | tf_op jit(solution)/shard_map/pallas_call | solution.py:490
  51.1 1.0 %collective-permute-start.16 = (f32[256,128]{1,0:T(8,128)S(1)}, f32[256,128]{1,0:T(8,128)S(1)}, u32[]{:S(2)}, u32[]{:S(2)}) collective-permute-start(f32[256,128]{1,0:T(8,128)S(1)} %get-tuple-element.57), channel_id=1, source_target_pairs={{0,8},{8,0},{16,24},{24,16},{1,9},{9,1},{17,25},{25,17},{2,10},{10... | collective-permute-start | bytes 393224 | tf_op jit(solution)/shard_map/ppermute | solution.py:353
  52.1 1.2 %collective-permute-start.18 = (f32[256,128]{1,0:T(8,128)S(1)}, f32[256,128]{1,0:T(8,128)S(1)}, u32[]{:S(2)}, u32[]{:S(2)}) collective-permute-start(f32[256,128]{1,0:T(8,128)S(1)} %mul.28.after), channel_id=1, source_target_pairs={{0,16},{8,24},{16,0},{24,8},{1,17},{9,25},{17,1},{25,9},{2,18},{10... | collective-permute-start | bytes 393224 | tf_op jit(solution)/shard_map/ppermute | solution.py:353
  53.4 1.0 %collective-permute-start.17 = (f32[256,128]{1,0:T(8,128)S(1)}, f32[256,128]{1,0:T(8,128)S(1)}, u32[]{:S(2)}, u32[]{:S(2)}) collective-permute-start(f32[256,128]{1,0:T(8,128)S(1)} %mul.29), channel_id=1, source_target_pairs={{0,16},{8,24},{16,0},{24,8},{1,17},{9,25},{17,1},{25,9},{2,18},{10... | collective-permute-start | bytes 393224 | tf_op jit(solution)/shard_map/ppermute | solution.py:353
  54.4 2.7 %collective-permute-done.18 = f32[256,128]{1,0:T(8,128)S(1)} collective-permute-done((f32[256,128]{1,0:T(8,128)S(1)}, f32[256,128]{1,0:T(8,128)S(1)}, u32[]{:S(2)}, u32[]{:S(2)}) %collective-permute-start.18) | collective-permute-done | bytes 131104 | tf_op jit(solution)/shard_map/ppermute | solution.py:353
  57.1 1.5 %collective-permute-start.20 = (f32[256,128]{1,0:T(8,128)S(1)}, f32[256,128]{1,0:T(8,128)S(1)}, u32[]{:S(2)}, u32[]{:S(2)}) collective-permute-start(f32[256,128]{1,0:T(8,128)S(1)} %bitcast_multiply_fusion.1), channel_id=1, source_target_pairs={{0,8},{8,0},{16,24},{24,16},{1,9},{9,1},{17,25},{25,17},{2,10},{10... | collective-permute-start | bytes 393224 | tf_op jit(solution)/shard_map/ppermute | solution.py:353
  58.7 1.2 %collective-permute-done.17 = f32[256,128]{1,0:T(8,128)S(1)} collective-permute-done((f32[256,128]{1,0:T(8,128)S(1)}, f32[256,128]{1,0:T(8,128)S(1)}, u32[]{:S(2)}, u32[]{:S(2)}) %collective-permute-start.17) | collective-permute-done | bytes 131104 | tf_op jit(solution)/shard_map/ppermute | solution.py:353
  60.0 1.0 %collective-permute-start.19 = (f32[256,128]{1,0:T(8,128)S(1)}, f32[256,128]{1,0:T(8,128)S(1)}, u32[]{:S(2)}, u32[]{:S(2)}) collective-permute-start(f32[256,128]{1,0:T(8,128)S(1)} %bitcast_multiply_fusion), channel_id=1, source_target_pairs={{0,8},{8,0},{16,24},{24,16},{1,9},{9,1},{17,25},{25,17},{2,10},{10... | collective-permute-start | bytes 393224 | tf_op jit(solution)/shard_map/ppermute | solution.py:353
  61.0 0.7 %shard_map.99.refs_1_ = f32[64,16,128]{2,1,0:T(8,128)} custom-call(f32[32,8,128]{2,1,0:T(8,128)S(1)} %bitcast.13, f32[32,8,128]{2,1,0:T(8,128)S(1)} %bitcast.15), custom_call_target="tpu_custom_call" | custom-call | flops 4194304 | bytes 1048576 | tf_op jit(solution)/shard_map/pallas_call | solution.py:349
  61.7 0.7 %shard_map.100.refs_1_ = f32[64,16,128]{2,1,0:T(8,128)} custom-call(f32[32,8,128]{2,1,0:T(8,128)S(1)} %bitcast.12, f32[64,16,128]{2,1,0:T(8,128)} %shard_map.99.refs_1_), custom_call_target="tpu_custom_call", output_to_operand_aliasing={{}: (1, {})} | custom-call | flops 4194304 | bytes 1048576 | tf_op jit(solution)/shard_map/pallas_call | solution.py:349
  62.4 0.7 %shard_map.101 = f32[64,16,128]{2,1,0:T(8,128)} custom-call(f32[32,8,128]{2,1,0:T(8,128)S(1)} %bitcast.14, f32[64,16,128]{2,1,0:T(8,128)} %shard_map.100.refs_1_), custom_call_target="tpu_custom_call", output_to_operand_aliasing={{}: (1, {})} | custom-call | flops 4194304 | bytes 1048576 | tf_op jit(solution)/shard_map/pallas_call | solution.py:349
  (33 shorter events, 2.0 us)
Async XLA Ops:
  0.0 1.9 %copy-start = (f32[64,16,128]{2,1,0:T(8,128)S(1)}, f32[64,16,128]{2,1,0:T(8,128)}, u32[]{:S(2)}) copy-start(f32[64,16,128]{2,1,0:T(8,128)} %param.9) | copy-start | bytes 1572868
  2.2 21.3 %collective-permute-start.7 = (f32[8,64,128]{2,1,0:T(8,128)S(1)}, f32[8,64,128]{2,1,0:T(8,128)S(1)}, u32[]{:S(2)}, u32[]{:S(2)}) collective-permute-start(f32[8,64,128]{2,1,0:T(8,128)S(1)} %get-tuple-element.42), channel_id=1, source_target_pairs={{0,1},{1,0},{2,3},{3,2},{4,5},{5,4},{6,7},{7,6},{8,9},{9,8},{10,11... | collective-permute-start | bytes 786440 | tf_op jit(solution)/shard_map/ppermute | solution.py:369
  2.5 19.3 %collective-permute-start = (f32[264,128]{1,0:T(8,128)S(1)}, f32[264,128]{1,0:T(8,128)S(1)}, u32[]{:S(2)}, u32[]{:S(2)}) collective-permute-start(f32[264,128]{1,0:T(8,128)S(1)} %get-tuple-element.33), channel_id=1, source_target_pairs={{0,7},{1,6},{2,5},{3,4},{4,3},{5,2},{6,1},{7,0},{8,15},{9,14},{10,... | collective-permute-start | bytes 405512 | tf_op jit(solution)/shard_map/ppermute | solution.py:441
  4.7 18.6 %collective-permute-start.1 = (f32[264,128]{1,0:T(8,128)S(1)}, f32[264,128]{1,0:T(8,128)S(1)}, u32[]{:S(2)}, u32[]{:S(2)}) collective-permute-start(f32[264,128]{1,0:T(8,128)S(1)} %get-tuple-element.34), channel_id=1, source_target_pairs={{0,6},{1,7},{2,4},{3,5},{4,2},{5,3},{6,0},{7,1},{8,14},{9,15},{10,... | collective-permute-start | bytes 405512 | tf_op jit(solution)/shard_map/ppermute | solution.py:441
  4.9 9.2 %collective-permute-start.8 = (f32[16,8,128]{2,1,0:T(8,128)S(1)}, f32[16,8,128]{2,1,0:T(8,128)S(1)}, u32[]{:S(2)}, u32[]{:S(2)}) collective-permute-start(f32[16,8,128]{2,1,0:T(8,128)S(1)} %get-tuple-element.43), channel_id=1, source_target_pairs={{0,2},{2,0},{4,6},{6,4},{1,3},{3,1},{5,7},{7,5},{8,10},{10,8},{12,... | collective-permute-start | bytes 196616 | tf_op jit(solution)/shard_map/ppermute | solution.py:369
  6.9 11.3 %collective-permute-start.9 = (f32[16,8,128]{2,1,0:T(8,128)S(1)}, f32[16,8,128]{2,1,0:T(8,128)S(1)}, u32[]{:S(2)}, u32[]{:S(2)}) collective-permute-start(f32[16,8,128]{2,1,0:T(8,128)S(1)} %get-tuple-element.44), channel_id=1, source_target_pairs={{2,4},{4,2},{3,5},{5,3},{10,12},{12,10},{11,13},{13,11},{18,20},{2... | collective-permute-start | bytes 196616 | tf_op jit(solution)/shard_map/ppermute | solution.py:369
  18.2 3.1 %collective-permute-start.10 = (f32[2,8,8,128]{3,2,1,0:T(8,128)S(1)}, f32[2,8,8,128]{3,2,1,0:T(8,128)S(1)}, u32[]{:S(2)}, u32[]{:S(2)}) collective-permute-start(f32[2,8,8,128]{3,2,1,0:T(8,128)S(1)} %shard_map.93), channel_id=1, source_target_pairs={{0,1},{1,0},{2,3},{3,2},{4,5},{5,4},{6,7},{7,6},{8,9},{9,8},{10,11... | collective-permute-start | bytes 196616 | tf_op jit(solution)/shard_map/ppermute | solution.py:369
  18.3 9.4 %collective-permute-start.2 = (f32[264,128]{1,0:T(8,128)S(1)}, f32[264,128]{1,0:T(8,128)S(1)}, u32[]{:S(2)}, u32[]{:S(2)}) collective-permute-start(f32[264,128]{1,0:T(8,128)S(1)} %get-tuple-element.35), channel_id=1, source_target_pairs={{0,5},{1,4},{2,7},{3,6},{4,1},{5,0},{6,3},{7,2},{8,13},{9,12},{10,... | collective-permute-start | bytes 405512 | tf_op jit(solution)/shard_map/ppermute | solution.py:441
  21.3 8.0 %collective-permute-start.3 = (f32[264,128]{1,0:T(8,128)S(1)}, f32[264,128]{1,0:T(8,128)S(1)}, u32[]{:S(2)}, u32[]{:S(2)}) collective-permute-start(f32[264,128]{1,0:T(8,128)S(1)} %get-tuple-element.36), channel_id=1, source_target_pairs={{0,4},{1,5},{2,6},{3,7},{4,0},{5,1},{6,2},{7,3},{8,12},{9,13},{10,... | collective-permute-start | bytes 405512 | tf_op jit(solution)/shard_map/ppermute | solution.py:441
  21.8 7.8 %collective-permute-start.4 = (f32[264,128]{1,0:T(8,128)S(1)}, f32[264,128]{1,0:T(8,128)S(1)}, u32[]{:S(2)}, u32[]{:S(2)}) collective-permute-start(f32[264,128]{1,0:T(8,128)S(1)} %get-tuple-element.37), channel_id=1, source_target_pairs={{0,3},{1,2},{2,1},{3,0},{4,7},{5,6},{6,5},{7,4},{8,11},{9,10},{10,... | collective-permute-start | bytes 405512 | tf_op jit(solution)/shard_map/ppermute | solution.py:441
  23.4 8.2 %collective-permute-start.5 = (f32[264,128]{1,0:T(8,128)S(1)}, f32[264,128]{1,0:T(8,128)S(1)}, u32[]{:S(2)}, u32[]{:S(2)}) collective-permute-start(f32[264,128]{1,0:T(8,128)S(1)} %get-tuple-element.38), channel_id=1, source_target_pairs={{0,2},{1,3},{2,0},{3,1},{4,6},{5,7},{6,4},{7,5},{8,10},{9,11},{10,... | collective-permute-start | bytes 405512 | tf_op jit(solution)/shard_map/ppermute | solution.py:441
  23.5 1.2 %copy-start.1 = (f32[1,17]{1,0:T(1,128)S(1)}, f32[1,17]{1,0:T(1,128)}, u32[]{:S(2)}) copy-start(f32[1,17]{1,0:T(1,128)} %refs_4_.3) | copy-start | bytes 208
  23.5 1.2 %copy-start.2 = (f32[1,17]{1,0:T(1,128)S(1)}, f32[1,17]{1,0:T(1,128)}, u32[]{:S(2)}) copy-start(f32[1,17]{1,0:T(1,128)} %refs_5_.1) | copy-start | bytes 208
  23.5 1.2 %copy-start.3 = (f32[1,33]{1,0:T(1,128)S(1)}, f32[1,33]{1,0:T(1,128)}, u32[]{:S(2)}) copy-start(f32[1,33]{1,0:T(1,128)} %refs_6_.1) | copy-start | bytes 400
  23.5 8.1 %collective-permute-start.6 = (f32[264,128]{1,0:T(8,128)S(1)}, f32[264,128]{1,0:T(8,128)S(1)}, u32[]{:S(2)}, u32[]{:S(2)}) collective-permute-start(f32[264,128]{1,0:T(8,128)S(1)} %get-tuple-element.39), channel_id=1, source_target_pairs={{0,1},{1,0},{2,3},{3,2},{4,5},{5,4},{6,7},{7,6},{8,9},{9,8},{10,11... | collective-permute-start | bytes 405512 | tf_op jit(solution)/shard_map/ppermute | solution.py:441
  32.7 17.5 %collective-permute-start.14 = (f32[8,64,128]{2,1,0:T(8,128)S(1)}, f32[8,64,128]{2,1,0:T(8,128)S(1)}, u32[]{:S(2)}, u32[]{:S(2)}) collective-permute-start(f32[8,64,128]{2,1,0:T(8,128)S(1)} %get-tuple-element.55), channel_id=1, source_target_pairs={{0,1},{1,0},{2,3},{3,2},{4,5},{5,4},{6,7},{7,6},{8,9},{9,8},{10,11... | collective-permute-start | bytes 786440 | tf_op jit(solution)/shard_map/ppermute | solution.py:369
  33.9 3.2 %collective-permute-start.11 = (f32[16,8,128]{2,1,0:T(8,128)S(1)}, f32[16,8,128]{2,1,0:T(8,128)S(1)}, u32[]{:S(2)}, u32[]{:S(2)}) collective-permute-start(f32[16,8,128]{2,1,0:T(8,128)S(1)} %get-tuple-element.47), channel_id=1, source_target_pairs={{0,2},{2,0},{4,6},{6,4},{1,3},{3,1},{5,7},{7,5},{8,10},{10,8},{12,... | collective-permute-start | bytes 196616 | tf_op jit(solution)/shard_map/ppermute | solution.py:369
  34.3 5.3 %collective-permute-start.12 = (f32[16,8,128]{2,1,0:T(8,128)S(1)}, f32[16,8,128]{2,1,0:T(8,128)S(1)}, u32[]{:S(2)}, u32[]{:S(2)}) collective-permute-start(f32[16,8,128]{2,1,0:T(8,128)S(1)} %get-tuple-element.48), channel_id=1, source_target_pairs={{2,4},{4,2},{3,5},{5,3},{10,12},{12,10},{11,13},{13,11},{18,20},{2... | collective-permute-start | bytes 196616 | tf_op jit(solution)/shard_map/ppermute | solution.py:369
  40.7 6.9 %collective-permute-start.13 = (f32[256,128]{1,0:T(8,128)S(1)}, f32[256,128]{1,0:T(8,128)S(1)}, u32[]{:S(2)}, u32[]{:S(2)}) collective-permute-start(f32[256,128]{1,0:T(8,128)S(1)} %get-tuple-element.53), channel_id=1, source_target_pairs={{0,8},{8,0},{16,24},{24,16},{1,9},{9,1},{17,25},{25,17},{2,10},{10... | collective-permute-start | bytes 393224 | tf_op jit(solution)/shard_map/ppermute | solution.py:353
  46.6 3.6 %collective-permute-start.15 = (f32[2,8,8,128]{3,2,1,0:T(8,128)S(1)}, f32[2,8,8,128]{3,2,1,0:T(8,128)S(1)}, u32[]{:S(2)}, u32[]{:S(2)}) collective-permute-start(f32[2,8,8,128]{3,2,1,0:T(8,128)S(1)} %shard_map.97), channel_id=1, source_target_pairs={{0,1},{1,0},{2,3},{3,2},{4,5},{5,4},{6,7},{7,6},{8,9},{9,8},{10,11... | collective-permute-start | bytes 196616 | tf_op jit(solution)/shard_map/ppermute | solution.py:369
  51.1 2.2 %collective-permute-start.16 = (f32[256,128]{1,0:T(8,128)S(1)}, f32[256,128]{1,0:T(8,128)S(1)}, u32[]{:S(2)}, u32[]{:S(2)}) collective-permute-start(f32[256,128]{1,0:T(8,128)S(1)} %get-tuple-element.57), channel_id=1, source_target_pairs={{0,8},{8,0},{16,24},{24,16},{1,9},{9,1},{17,25},{25,17},{2,10},{10... | collective-permute-start | bytes 393224 | tf_op jit(solution)/shard_map/ppermute | solution.py:353
  52.1 5.0 %collective-permute-start.18 = (f32[256,128]{1,0:T(8,128)S(1)}, f32[256,128]{1,0:T(8,128)S(1)}, u32[]{:S(2)}, u32[]{:S(2)}) collective-permute-start(f32[256,128]{1,0:T(8,128)S(1)} %mul.28.after), channel_id=1, source_target_pairs={{0,16},{8,24},{16,0},{24,8},{1,17},{9,25},{17,1},{25,9},{2,18},{10... | collective-permute-start | bytes 393224 | tf_op jit(solution)/shard_map/ppermute | solution.py:353
  53.4 6.6 %collective-permute-start.17 = (f32[256,128]{1,0:T(8,128)S(1)}, f32[256,128]{1,0:T(8,128)S(1)}, u32[]{:S(2)}, u32[]{:S(2)}) collective-permute-start(f32[256,128]{1,0:T(8,128)S(1)} %mul.29), channel_id=1, source_target_pairs={{0,16},{8,24},{16,0},{24,8},{1,17},{9,25},{17,1},{25,9},{2,18},{10... | collective-permute-start | bytes 393224 | tf_op jit(solution)/shard_map/ppermute | solution.py:353
  57.1 3.8 %collective-permute-start.20 = (f32[256,128]{1,0:T(8,128)S(1)}, f32[256,128]{1,0:T(8,128)S(1)}, u32[]{:S(2)}, u32[]{:S(2)}) collective-permute-start(f32[256,128]{1,0:T(8,128)S(1)} %bitcast_multiply_fusion.1), channel_id=1, source_target_pairs={{0,8},{8,0},{16,24},{24,16},{1,9},{9,1},{17,25},{25,17},{2,10},{10... | collective-permute-start | bytes 393224 | tf_op jit(solution)/shard_map/ppermute | solution.py:353
  60.0 2.4 %collective-permute-start.19 = (f32[256,128]{1,0:T(8,128)S(1)}, f32[256,128]{1,0:T(8,128)S(1)}, u32[]{:S(2)}, u32[]{:S(2)}) collective-permute-start(f32[256,128]{1,0:T(8,128)S(1)} %bitcast_multiply_fusion), channel_id=1, source_target_pairs={{0,8},{8,0},{16,24},{24,16},{1,9},{9,1},{17,25},{25,17},{2,10},{10... | collective-permute-start | bytes 393224 | tf_op jit(solution)/shard_map/ppermute | solution.py:353

commit v2 on v1

--- a/solution.py
+++ b/solution.py
@@ -28,7 +28,6 @@
 TAPS = 2 * R + 1
 ROWS = 24
 PACK_LIMIT = 32 << 20
-BLUR_LIMIT = 32 << 20
 GROUP = 64
 CHUNK = YP * GROUP + 8
 
@@ -149,10 +148,22 @@
         out[1] = xb[rows]
 
 
-def turn_kernel(estimate, after, turned, *edges):
+def turn_kernel(estimate, after, turned, edge_x, *edges_y):
     for y in range(CY):
         turned[y] = estimate[pl.ds(y, CX, stride=CY), :]
-    put_edges(turned, edges)
+    odd_x, odd_y = sides()
+    core = lax.axis_index("view") % 2
+    at = jnp.where(core == 0, 1 - odd_x, odd_x) * (CX - R)
+    edge_x[...] = turned[:, pl.ds(pl.multiple_of(at, R), R), :]
+    for phase, out in enumerate(edges_y):
+        at = (odd_y if phase else 1 - odd_y) * (CY - R) + core * (R // 2)
+        out[...] = turned[pl.ds(at, R // 2)]
+
+
+def cut_kernel(got, *outs):
+    _, odd_y = sides()
+    for phase, out in enumerate(outs):
+        out[...] = got[pl.ds((odd_y if phase else 1 - odd_y) * (CY - R), R)]
 
 
 def total(kernel, taps):
@@ -162,7 +173,7 @@
     return acc
 
 
-def make_bands(kx, ky, kz, *outs):
+def band_kernel(kx, ky, kz, *outs):
     ztaps = 2 * RZ + 1
     for reverse in range(2):
         band_x, band_z, taps = outs[3 * reverse : 3 * reverse + 3]
@@ -220,20 +231,34 @@
     return [result[y * CX : (y + 1) * CX] for y in range(HY)]
 
 
-def put_x(own, xa, xb, padded, count):
+def put_x(xa, xb, padded, count, shared=False):
     odd_x, _ = sides()
-    padded[:count, R : R + CX, :] = own[...]
-    padded[:count, pl.ds(pl.multiple_of((1 - odd_x) * (CX + R), R), R), :] = xa[...]
-    padded[:count, pl.ds(pl.multiple_of(odd_x * (CX + R), R), R), :] = xb[...]
-
-
-def far_lines(own, x_halos, y_halo, band_x, padded, lines):
-    _, odd_y = sides()
-    put_x(own, *x_halos, padded, CY)
+    first = 1 - odd_x
+    if shared:
+        first = jnp.where(lax.axis_index("view") % 2 == 0, first, odd_x)
+    padded[:count, pl.ds(pl.multiple_of(first * (CX + R), R), R), :] = xa[...]
+    padded[:count, pl.ds(pl.multiple_of((1 - first) * (CX + R), R), R), :] = xb[...]
+
+
+def put_side(y_halo, padded):
+    if len(y_halo) == 2:
+        padded[:R, R : R + CX, :] = y_halo[0][...]
+        put_x(y_halo[1].at[0], y_halo[1].at[1], padded, R)
+    else:
+        core = lax.axis_index("view") % 2
+        padded[pl.ds(core * (R // 2), R // 2), R : R + CX, :] = y_halo[0][...]
+        padded[pl.ds((1 - core) * (R // 2), R // 2), R : R + CX, :] = y_halo[1][...]
+        put_x(*y_halo[2:], padded, R, shared=True)
+
+
+def far_lines(own, x_halos, y_halo, band_x, padded, lines, shared=False):
+    _, odd_y = sides()
+    padded[:, R : R + CX, :] = own[...]
+    put_x(*x_halos, padded, CY, shared)
     smear_x(padded, CY, band_x, lines, R)
     far = (CY + R) * odd_y
     if y_halo:
-        put_x(y_halo[0], y_halo[1].at[0], y_halo[1].at[1], padded, R)
+        put_side(y_halo, padded)
         smear_x(padded, R, band_x, lines, far)
     else:
         lines[pl.ds(far, R)] = jnp.zeros((R, CX, CZ), F32)
@@ -241,19 +266,28 @@
 
 def near_lines(y_halo, band_x, padded, lines):
     _, odd_y = sides()
-    put_x(y_halo[0], y_halo[1].at[0], y_halo[1].at[1], padded, R)
+    put_side(y_halo, padded)
     smear_x(padded, R, band_x, lines, (CY + R) * (1 - odd_y))
 
 
-def blur_kernel(own, *refs):
-    halos, (kx, ky, kz, out, *bands) = refs[:-13], refs[-13:]
-    band_x, band_z, taps, padded, lines, held = bands[3:]
-    make_bands(kx, ky, kz, *bands[3:6], *bands[:3])
-    far_lines(own, halos[-2:], halos[2:-2], band_x, padded, lines)
-    near_lines(halos[:2], band_x, padded, lines)
-    for start in range(0, CY, HY):
-        for y, value in enumerate(smear_yz(lines, start, taps, band_z, held)):
-            out[start + y] = value
+def blur_far_kernel(own, *refs):
+    ins, (out, lines, padded, held) = refs[:-4], refs[-4:]
+    halos, (band_x, band_z, taps) = ins[:-3], ins[-3:]
+    _, odd_y = sides()
+    far_lines(own, halos[:2], halos[2:], band_x, padded, lines, shared=True)
+    for y, value in enumerate(smear_yz(lines, HY * odd_y, taps, band_z, held)):
+        out[y] = value
+
+
+def blur_near_kernel(far, before, *refs):
+    y_halo, (band_x, band_z, taps, out, padded, held, lines) = refs[:4], refs[4:]
+    _, odd_y = sides()
+    lines[R : R + CY] = before[R : R + CY]
+    near_lines(y_halo, band_x, padded, lines)
+    out[pl.ds(HY * odd_y, HY)] = far[...]
+    start = HY * (1 - odd_y)
+    for y, value in enumerate(smear_yz(lines, start, taps, band_z, held)):
+        out[start + y] = value
 
 
 def put_quarters(values, mine, other, whole):
@@ -298,7 +332,7 @@
     keep = jnp.where(iota((CZ, rows), 0) < count, weight, 0.0).T
 
     def gathered(values):
-        return sum(mm(chooser, part) for part in three(values))
+        return sum(mm(chooser, part) for part in two(values))
 
     cover = gathered(keep)
     for j in range(0, YP, 2):
@@ -375,6 +409,26 @@
     return [value for both in zip(got_y, got_c) for value in both] + got_x
 
 
+def shared_halo(edge_x, edges_y):
+    x_pairs, y_pairs, wide = pairs("bx"), pairs("by"), lax.axis_size("bx")
+    x_pairs = x_pairs + [[]] * (2 - len(x_pairs))
+    moves = [
+        (view * wide + a, view * wide + b)
+        for view in range(lax.axis_size("view"))
+        for a, b in x_pairs[view % 2]
+    ]
+    got_x = lax.ppermute(edge_x, ("view", "bx"), moves)
+    got_y = []
+    for edge, pair in zip(edges_y, y_pairs):
+        got_y.append(lax.ppermute(edge, "by", pair))
+    cut = call(cut_kernel, [(R, R, CZ)] * len(y_pairs), in_specs=[VM])(got_x)
+    out = [got_x, swap(got_x, "view", 1)]
+    for y, corner, pair in zip(got_y, cut, y_pairs):
+        corner = lax.ppermute(corner, "by", pair)
+        out += [y, swap(y, "view", 1), corner, swap(corner, "view", 1)]
+    return out
+
+
 def generic_exchange(bricks, observed, target, slot, count, weight):
     capacity = max(4, 2 * PIECES // bricks)
     member = (target[:, None] == jnp.arange(bricks)[None, :]).astype(jnp.int32)
@@ -414,7 +468,8 @@
     phases = len(pairs("by"))
     flat = estimate.reshape(CX * CY, CZ)
     edge_shapes = [(R, CX, CZ)] * phases + [(CY, R, CZ)] * 2
-    brick, quarter, lines = (CY, CX, CZ), (HX * HY, CZ), (CY + 2 * R, CX, CZ)
+    brick, half = (CY, CX, CZ), (HY, CX, CZ)
+    quarter, lines = (HX * HY, CZ), (CY + 2 * R, CX, CZ)
     padded, held = pltpu.VMEM((CY, XE, CZ), F32), pltpu.VMEM((HY, CX, CZ), F32)
     whole = pltpu.VMEM((CX * HY, CZ), F32)
 
@@ -450,14 +505,20 @@
             blend_weight[0],
         )
 
-    turned, *edges = call(turn_kernel, [brick] + edge_shapes, in_specs=[VM, ANY])(flat, token)
-    around = halo(edges)
-    bands = [((CX, 3 * XE), BF16), ((3 * CZ, CZ), BF16), ((ROWS, CZ), F32)]
-    work = [pltpu.VMEM(*band) for band in bands] + [padded, pltpu.VMEM(lines, F32), held]
-    shapes = [brick] + [jax.ShapeDtypeStruct(*band) for band in bands]
-    specs = [VM] * (len(around) + 1) + [SM] * 3
-    blurred, *bands = call(blur_kernel, shapes, work, specs, limit=BLUR_LIMIT)(
-        turned, *around, kernel_x, kernel_y, kernel_z
+    shapes = [brick, (CY, R, CZ)] + [(R // 2, CX, CZ)] * phases
+    turned, edge_x, *edges_y = call(turn_kernel, shapes, in_specs=[VM, ANY])(flat, token)
+    around = shared_halo(edge_x, edges_y)
+    shapes = [((CX, 3 * XE), BF16), ((3 * CZ, CZ), BF16), ((ROWS, CZ), F32)] * 2
+    shapes = [jax.ShapeDtypeStruct(*shape) for shape in shapes]
+    bands = call(band_kernel, shapes, in_specs=[SM] * 3)(kernel_x, kernel_y, kernel_z)
+    forward, bands = bands[:3], bands[3:]
+    far_halos, near_halos = around[:2] + around[6:], around[2:6]
+    blurred, before = call(
+        blur_far_kernel, [half, lines], [padded, held], [VM] * (len(far_halos) + 4)
+    )(turned, *far_halos, *forward)
+    work = [padded, held, pltpu.VMEM(lines, F32)]
+    (blurred,) = call(blur_near_kernel, [brick], work, [VM] * 9)(
+        blurred, before, *near_halos, *forward
     )
 
     def ratios(*refs):

time: 63.3 us -> 65.6 us (1.036)
  the two profiles are of different devices: /device:TPU:13 before, /device:TPU:9 now
where the time goes in v2:
time: 65.6 us; the launch traced here: 65.4 us
  starting transfers between devices  28.5 us (43%)
  waiting for transfers between devices  26.4 us (40%)
  Pallas kernels  10.3 us (16%)
    ppermute x9, starting transfers between devices, swap(): lax.ppermute(x, axis, [(i, i ^ mask) for i in range(lax.axis_size(axis))])  12.8 us
    ppermute x1, waiting for transfers between devices, shared_halo(): got_x = lax.ppermute(edge_x, ('view', 'bx'), moves)  7.64 us
    ppermute x7, starting transfers between devices, local(): chunks.append(lax.ppermute(packed[s], ('bx', 'by'), pair))  6.72 us
    ppermute x7, waiting for transfers between devices, local(): chunks.append(lax.ppermute(packed[s], ('bx', 'by'), pair))  6.16 us
    ppermute x9, waiting for transfers between devices, swap(): lax.ppermute(x, axis, [(i, i ^ mask) for i in range(lax.axis_size(axis))])  5.82 us
    ppermute x4, waiting for transfers between devices, move(): return lax.ppermute(value, axis, moves) if moves else jnp.zeros_like(value)  5.35 us
    ppermute x1, starting transfers between devices, shared_halo(): got_x = lax.ppermute(edge_x, ('view', 'bx'), moves)  3.2 us
    ppermute x4, starting transfers between devices, move(): return lax.ppermute(value, axis, moves) if moves else jnp.zeros_like(value)  3.1 us
  transfers between devices with their start and end apart: 23, of which 12 were waited for; matrix products, arithmetic and copies ran while one was open for 0% of the time, Pallas kernels for 9%

profile of v2, /device:TPU:9, one launch (start us, length us, event | category | flops | bytes accessed | tf_op | source)
XLA Modules:
  0.0 65.4 jit_solution(2881545468001755056)
XLA Ops:
  0.0 1.9 %shard_map.91 = (f32[264,128]{1,0:T(8,128)S(1)}, f32[264,128]{1,0:T(8,128)S(1)}, f32[264,128]{1,0:T(8,128)S(1)}, f32[264,128]{1,0:T(8,128)S(1)}, f32[264,128]{1,...) custom-call(f32[256,512]{1,0:T(8,128)} %bitcast.16, ...), custom_call_target="tpu_custom_call" | custom-call | flops 4194304 | bytes 1048576 | tf_op jit(solution)/shard_map/pallas_call | solution.py:481
  2.2 1.3 %collective-permute-start.9 = (f32[4,64,128]{2,1,0:T(8,128)S(1)}, f32[4,64,128]{2,1,0:T(8,128)S(1)}, u32[]{:S(2)}, u32[]{:S(2)}) collective-permute-start(f32[4,64,128]{2,1,0:T(8,128)S(1)} %get-tuple-element.51), channel_id=1, source_target_pairs={{0,1},{1,0},{2,3},{3,2},{4,5},{5,4},{6,7},{7,6},{8,9},{9,8},{10,11... | collective-permute-start | bytes 393224 | tf_op jit(solution)/shard_map/ppermute | solution.py:423
  3.5 1.2 %collective-permute-start = (f32[264,128]{1,0:T(8,128)S(1)}, f32[264,128]{1,0:T(8,128)S(1)}, u32[]{:S(2)}, u32[]{:S(2)}) collective-permute-start(f32[264,128]{1,0:T(8,128)S(1)} %get-tuple-element.36), channel_id=1, source_target_pairs={{0,7},{1,6},{2,5},{3,4},{4,3},{5,2},{6,1},{7,0},{8,15},{9,14},{10,... | collective-permute-start | bytes 405512 | tf_op jit(solution)/shard_map/ppermute | solution.py:496
  4.9 3.2 %collective-permute-start.7 = (f32[16,8,128]{2,1,0:T(8,128)S(1)}, f32[16,8,128]{2,1,0:T(8,128)S(1)}, u32[]{:S(2)}, u32[]{:S(2)}) collective-permute-start(f32[16,8,128]{2,1,0:T(8,128)S(1)} %get-tuple-element.45), channel_id=1, source_target_pairs={{0,2},{2,0},{4,6},{6,4},{10,12},{12,10},{16,18},{18,16},{20,22},{2... | collective-permute-start | bytes 196616 | tf_op jit(solution)/shard_map/ppermute | solution.py:420
  8.1 2.4 %collective-permute-start.10 = (f32[4,64,128]{2,1,0:T(8,128)S(1)}, f32[4,64,128]{2,1,0:T(8,128)S(1)}, u32[]{:S(2)}, u32[]{:S(2)}) collective-permute-start(f32[4,64,128]{2,1,0:T(8,128)S(1)} %collective-permute-done.9.refs_0_), channel_id=1, source_target_pairs={{0,8},{8,0},{16,24},{24,16},{1,9},{9,1},{17,25},{25,17},{2,10},{10... | collective-permute-start | bytes 393224 | tf_op jit(solution)/shard_map/ppermute | solution.py:387
  10.4 7.6 %collective-permute-done.7.refs_0_.got = f32[16,8,128]{2,1,0:T(8,128)S(1)} collective-permute-done((f32[16,8,128]{2,1,0:T(8,128)S(1)}, f32[16,8,128]{2,1,0:T(8,128)S(1)}, u32[]{:S(2)}, u32[]{:S(2)}) %collective-permute-start.7) | collective-permute-done | bytes 65568 | tf_op jit(solution)/shard_map/ppermute | solution.py:420
  18.1 1.4 %collective-permute-start.11 = (f32[8,8,128]{2,1,0:T(8,128)S(1)}, f32[8,8,128]{2,1,0:T(8,128)S(1)}, u32[]{:S(2)}, u32[]{:S(2)}) collective-permute-start(f32[8,8,128]{2,1,0:T(8,128)S(1)} %shard_map.95), channel_id=1, source_target_pairs={{0,1},{1,0},{2,3},{3,2},{4,5},{5,4},{6,7},{7,6},{8,9},{9,8},{10,11... | collective-permute-start | bytes 98312 | tf_op jit(solution)/shard_map/ppermute | solution.py:427
  19.5 1.4 %collective-permute-done.11.refs_2_ = f32[8,8,128]{2,1,0:T(8,128)S(1)} collective-permute-done((f32[8,8,128]{2,1,0:T(8,128)S(1)}, f32[8,8,128]{2,1,0:T(8,128)S(1)}, u32[]{:S(2)}, u32[]{:S(2)}) %collective-permute-start.11) | collective-permute-done | bytes 32800 | tf_op jit(solution)/shard_map/ppermute | solution.py:427
  20.9 1.7 %collective-permute-start.12 = (f32[8,8,128]{2,1,0:T(8,128)S(1)}, f32[8,8,128]{2,1,0:T(8,128)S(1)}, u32[]{:S(2)}, u32[]{:S(2)}) collective-permute-start(f32[8,8,128]{2,1,0:T(8,128)S(1)} %collective-permute-done.11.refs_2_), channel_id=1, source_target_pairs={{0,8},{8,0},{16,24},{24,16},{1,9},{9,1},{17,25},{25,17},{2,10},{10... | collective-permute-start | bytes 98312 | tf_op jit(solution)/shard_map/ppermute | solution.py:387
  22.5 0.9 %collective-permute-done.12.refs_3_ = f32[8,8,128]{2,1,0:T(8,128)S(1)} collective-permute-done((f32[8,8,128]{2,1,0:T(8,128)S(1)}, f32[8,8,128]{2,1,0:T(8,128)S(1)}, u32[]{:S(2)}, u32[]{:S(2)}) %collective-permute-start.12) | collective-permute-done | bytes 32800 | tf_op jit(solution)/shard_map/ppermute | solution.py:387
  23.4 2.6 %collective-permute-start.3 = (f32[264,128]{1,0:T(8,128)S(1)}, f32[264,128]{1,0:T(8,128)S(1)}, u32[]{:S(2)}, u32[]{:S(2)}) collective-permute-start(f32[264,128]{1,0:T(8,128)S(1)} %get-tuple-element.39), channel_id=1, source_target_pairs={{0,4},{1,5},{2,6},{3,7},{4,0},{5,1},{6,2},{7,3},{8,12},{9,13},{10,... | collective-permute-start | bytes 405512 | tf_op jit(solution)/shard_map/ppermute | solution.py:496
  27.3 1.4 %collective-permute-start.6 = (f32[264,128]{1,0:T(8,128)S(1)}, f32[264,128]{1,0:T(8,128)S(1)}, u32[]{:S(2)}, u32[]{:S(2)}) collective-permute-start(f32[264,128]{1,0:T(8,128)S(1)} %get-tuple-element.42), channel_id=1, source_target_pairs={{0,1},{1,0},{2,3},{3,2},{4,5},{5,4},{6,7},{7,6},{8,9},{9,8},{10,11... | collective-permute-start | bytes 405512 | tf_op jit(solution)/shard_map/ppermute | solution.py:496
  28.7 1.2 %shard_map.93 = (bf16[64,240]{1,0:T(8,128)(2,1)S(1)}, bf16[384,128]{1,0:T(8,128)(2,1)S(1)}, f32[24,128]{1,0:T(8,128)S(1)}, bf16[64,240]{1,0:T(8,128)(2,1)S(1)}, ...) custom-call(f32[1,17]{1,0:T(1,128)S(1)} %copy-done.1, f32[1,17]{1,0:T(1,128)S(1)} %copy-done.2, f32[1,33]{1,0:T(1,128)S(1)} %copy-done.3), custom_call_target="tpu_custom_call" | custom-call | flops 4194304 | bytes 1048576 | tf_op jit(solution)/shard_map/pallas_call | solution.py:513
  30.0 1.0 %shard_map.94 = (f32[8,64,128]{2,1,0:T(8,128)S(1)}, f32[32,64,128]{2,1,0:T(8,128)S(1)}) custom-call(f32[16,64,128]{2,1,0:T(8,128)S(1)} %get-tuple-element.44.own, f32[16,8,128]{2,1,0:T(8,128)S(1)} %collective-permute-done.7.refs_0_.got, f32[16,8,128]{2,1,0:T(8,128)S(1)} %collective-permute-done.8.refs_1_, ...), custom_call_target="tpu_custom_call" | custom-call | flops 4194304 | bytes 1048576 | tf_op jit(solution)/shard_map/pallas_call | solution.py:516
  31.0 1.0 %shard_map.96.refs_8_ = f32[16,64,128]{2,1,0:T(8,128)S(1)} custom-call(f32[8,64,128]{2,1,0:T(8,128)S(1)} %get-tuple-element.49.far, f32[32,64,128]{2,1,0:T(8,128)S(1)} %get-tuple-element.50.before, f32[4,64,128]{2,1,0:T(8,128)S(1)} %collective-permute-done.9.refs_0_, f32[4,64,128]{2,1,0:T(8,128)S(1)} %collective-permute-done.10.refs_1_, ...), custom_call_target="tpu_custom_call" | custom-call | flops 4194304 | bytes 1048576 | tf_op jit(solution)/shard_map/pallas_call | solution.py:520
  32.0 2.7 %collective-permute-done.3.refs_4_ = f32[264,128]{1,0:T(8,128)S(1)} collective-permute-done((f32[264,128]{1,0:T(8,128)S(1)}, f32[264,128]{1,0:T(8,128)S(1)}, u32[]{:S(2)}, u32[]{:S(2)}) %collective-permute-start.3) | collective-permute-done | bytes 135200 | tf_op jit(solution)/shard_map/ppermute | solution.py:496
  35.2 2.9 %collective-permute-done.5.refs_6_ = f32[264,128]{1,0:T(8,128)S(1)} collective-permute-done((f32[264,128]{1,0:T(8,128)S(1)}, f32[264,128]{1,0:T(8,128)S(1)}, u32[]{:S(2)}, u32[]{:S(2)}) %collective-permute-start.5) | collective-permute-done | bytes 135200 | tf_op jit(solution)/shard_map/ppermute | solution.py:496
  38.1 0.9 %shard_map.97 = (f32[16,64,128]{2,1,0:T(8,128)S(1)}, f32[8,64,128]{2,1,0:T(8,128)S(1)}, f32[16,8,128]{2,1,0:T(8,128)S(1)}, f32[16,8,128]{2,1,0:T(8,128)S(1)}) custom-call(f32[264,128]{1,0:T(8,128)S(1)} %get-tuple-element.35.refs_0_, f32[264,128]{1,0:T(8,128)S(1)} %collective-permute-done.refs_1_, f32[264,128]{1,0:T(8,128)S(1)} %collective-permute-done.1.refs_2_, ...), custom_call_target="tpu_custom_call" | custom-call | flops 4194304 | bytes 1048576 | tf_op jit(solution)/shard_map/pallas_call | solution.py:527
  39.6 2.5 %collective-permute-start.14 = (f32[16,8,128]{2,1,0:T(8,128)S(1)}, f32[16,8,128]{2,1,0:T(8,128)S(1)}, u32[]{:S(2)}, u32[]{:S(2)}) collective-permute-start(f32[16,8,128]{2,1,0:T(8,128)S(1)} %get-tuple-element.54), channel_id=1, source_target_pairs={{2,4},{4,2},{3,5},{5,3},{10,12},{12,10},{11,13},{13,11},{18,20},{2... | collective-permute-start | bytes 196616 | tf_op jit(solution)/shard_map/ppermute | solution.py:403
  42.4 2.5 %collective-permute-done.14.refs_1_.xb = f32[16,8,128]{2,1,0:T(8,128)S(1)} collective-permute-done((f32[16,8,128]{2,1,0:T(8,128)S(1)}, f32[16,8,128]{2,1,0:T(8,128)S(1)}, u32[]{:S(2)}, u32[]{:S(2)}) %collective-permute-start.14) | collective-permute-done | bytes 65568 | tf_op jit(solution)/shard_map/ppermute | solution.py:403
  44.9 1.0 %shard_map.98 = (f32[256,128]{1,0:T(8,128)S(1)}, f32[256,128]{1,0:T(8,128)S(1)}, f32[32,64,128]{2,1,0:T(8,128)S(1)}) custom-call(f32[16,64,128]{2,1,0:T(8,128)S(1)} %get-tuple-element.52.own, f32[16,8,128]{2,1,0:T(8,128)S(1)} %collective-permute-done.13.refs_0_.xa, f32[16,8,128]{2,1,0:T(8,128)S(1)} %collective-permute-done.14.refs_1_.xb, ...), custom_call_target="tpu_custom_call" | custom-call | flops 4194304 | bytes 1048576 | tf_op jit(solution)/shard_map/pallas_call | solution.py:532
  46.0 3.0 %collective-permute-start.15 = (f32[256,128]{1,0:T(8,128)S(1)}, f32[256,128]{1,0:T(8,128)S(1)}, u32[]{:S(2)}, u32[]{:S(2)}) collective-permute-start(f32[256,128]{1,0:T(8,128)S(1)} %get-tuple-element.59), channel_id=1, source_target_pairs={{0,8},{8,0},{16,24},{24,16},{1,9},{9,1},{17,25},{25,17},{2,10},{10... | collective-permute-start | bytes 393224 | tf_op jit(solution)/shard_map/ppermute | solution.py:387
  49.0 1.0 %collective-permute-done.15 = f32[256,128]{1,0:T(8,128)S(1)} collective-permute-done((f32[256,128]{1,0:T(8,128)S(1)}, f32[256,128]{1,0:T(8,128)S(1)}, u32[]{:S(2)}, u32[]{:S(2)}) %collective-permute-start.15) | collective-permute-done | bytes 131104 | tf_op jit(solution)/shard_map/ppermute | solution.py:387
  50.0 2.6 %collective-permute-done.17.refs_1_ = f32[2,8,8,128]{3,2,1,0:T(8,128)S(1)} collective-permute-done((f32[2,8,8,128]{3,2,1,0:T(8,128)S(1)}, f32[2,8,8,128]{3,2,1,0:T(8,128)S(1)}, u32[]{:S(2)}, u32[]{:S(2)}) %collective-permute-start.17) | collective-permute-done | bytes 65568 | tf_op jit(solution)/shard_map/ppermute | solution.py:403
  52.5 0.9 %shard_map.100 = (f32[256,128]{1,0:T(8,128)S(1)}, f32[256,128]{1,0:T(8,128)S(1)}) custom-call(f32[256,128]{1,0:T(8,128)S(1)} %mul.28.after, f32[32,64,128]{2,1,0:T(8,128)S(1)} %get-tuple-element.60.before, f32[8,64,128]{2,1,0:T(8,128)S(1)} %collective-permute-done.16.refs_0_, f32[2,8,8,128]{3,2,1,0:T(8,128)S(1)} %collective-permute-done.17.refs_1_, ...), custom_call_target="tpu_custom_call" | custom-call | flops 4194304 | bytes 1048576 | tf_op jit(solution)/shard_map/pallas_call | solution.py:551
  53.5 1.0 %collective-permute-start.18 = (f32[256,128]{1,0:T(8,128)S(1)}, f32[256,128]{1,0:T(8,128)S(1)}, u32[]{:S(2)}, u32[]{:S(2)}) collective-permute-start(f32[256,128]{1,0:T(8,128)S(1)} %get-tuple-element.63), channel_id=1, source_target_pairs={{0,8},{8,0},{16,24},{24,16},{1,9},{9,1},{17,25},{25,17},{2,10},{10... | collective-permute-start | bytes 393224 | tf_op jit(solution)/shard_map/ppermute | solution.py:387
  54.5 1.2 %collective-permute-start.20 = (f32[256,128]{1,0:T(8,128)S(1)}, f32[256,128]{1,0:T(8,128)S(1)}, u32[]{:S(2)}, u32[]{:S(2)}) collective-permute-start(f32[256,128]{1,0:T(8,128)S(1)} %mul.28.after), channel_id=1, source_target_pairs={{0,16},{8,24},{16,0},{24,8},{1,17},{9,25},{17,1},{25,9},{2,18},{10... | collective-permute-start | bytes 393224 | tf_op jit(solution)/shard_map/ppermute | solution.py:387
  55.7 1.0 %collective-permute-start.19 = (f32[256,128]{1,0:T(8,128)S(1)}, f32[256,128]{1,0:T(8,128)S(1)}, u32[]{:S(2)}, u32[]{:S(2)}) collective-permute-start(f32[256,128]{1,0:T(8,128)S(1)} %mul.29), channel_id=1, source_target_pairs={{0,16},{8,24},{16,0},{24,8},{1,17},{9,25},{17,1},{25,9},{2,18},{10... | collective-permute-start | bytes 393224 | tf_op jit(solution)/shard_map/ppermute | solution.py:387
  56.8 2.7 %collective-permute-done.20 = f32[256,128]{1,0:T(8,128)S(1)} collective-permute-done((f32[256,128]{1,0:T(8,128)S(1)}, f32[256,128]{1,0:T(8,128)S(1)}, u32[]{:S(2)}, u32[]{:S(2)}) %collective-permute-start.20) | collective-permute-done | bytes 131104 | tf_op jit(solution)/shard_map/ppermute | solution.py:387
  59.5 1.5 %collective-permute-start.22 = (f32[256,128]{1,0:T(8,128)S(1)}, f32[256,128]{1,0:T(8,128)S(1)}, u32[]{:S(2)}, u32[]{:S(2)}) collective-permute-start(f32[256,128]{1,0:T(8,128)S(1)} %bitcast_multiply_fusion.1), channel_id=1, source_target_pairs={{0,8},{8,0},{16,24},{24,16},{1,9},{9,1},{17,25},{25,17},{2,10},{10... | collective-permute-start | bytes 393224 | tf_op jit(solution)/shard_map/ppermute | solution.py:387
  61.1 1.2 %collective-permute-done.19 = f32[256,128]{1,0:T(8,128)S(1)} collective-permute-done((f32[256,128]{1,0:T(8,128)S(1)}, f32[256,128]{1,0:T(8,128)S(1)}, u32[]{:S(2)}, u32[]{:S(2)}) %collective-permute-start.19) | collective-permute-done | bytes 131104 | tf_op jit(solution)/shard_map/ppermute | solution.py:387
  62.3 1.0 %collective-permute-start.21 = (f32[256,128]{1,0:T(8,128)S(1)}, f32[256,128]{1,0:T(8,128)S(1)}, u32[]{:S(2)}, u32[]{:S(2)}) collective-permute-start(f32[256,128]{1,0:T(8,128)S(1)} %bitcast_multiply_fusion), channel_id=1, source_target_pairs={{0,8},{8,0},{16,24},{24,16},{1,9},{9,1},{17,25},{25,17},{2,10},{10... | collective-permute-start | bytes 393224 | tf_op jit(solution)/shard_map/ppermute | solution.py:387
  (39 shorter events, 5.4 us)
Async XLA Ops:
  0.0 1.9 %copy-start = (f32[64,16,128]{2,1,0:T(8,128)S(1)}, f32[64,16,128]{2,1,0:T(8,128)}, u32[]{:S(2)}) copy-start(f32[64,16,128]{2,1,0:T(8,128)} %param.9) | copy-start | bytes 1572868
  2.2 5.9 %collective-permute-start.9 = (f32[4,64,128]{2,1,0:T(8,128)S(1)}, f32[4,64,128]{2,1,0:T(8,128)S(1)}, u32[]{:S(2)}, u32[]{:S(2)}) collective-permute-start(f32[4,64,128]{2,1,0:T(8,128)S(1)} %get-tuple-element.51), channel_id=1, source_target_pairs={{0,1},{1,0},{2,3},{3,2},{4,5},{5,4},{6,7},{7,6},{8,9},{9,8},{10,11... | collective-permute-start | bytes 393224 | tf_op jit(solution)/shard_map/ppermute | solution.py:423
  3.5 22.5 %collective-permute-start = (f32[264,128]{1,0:T(8,128)S(1)}, f32[264,128]{1,0:T(8,128)S(1)}, u32[]{:S(2)}, u32[]{:S(2)}) collective-permute-start(f32[264,128]{1,0:T(8,128)S(1)} %get-tuple-element.36), channel_id=1, source_target_pairs={{0,7},{1,6},{2,5},{3,4},{4,3},{5,2},{6,1},{7,0},{8,15},{9,14},{10,... | collective-permute-start | bytes 405512 | tf_op jit(solution)/shard_map/ppermute | solution.py:496
  4.7 21.8 %collective-permute-start.1 = (f32[264,128]{1,0:T(8,128)S(1)}, f32[264,128]{1,0:T(8,128)S(1)}, u32[]{:S(2)}, u32[]{:S(2)}) collective-permute-start(f32[264,128]{1,0:T(8,128)S(1)} %get-tuple-element.37), channel_id=1, source_target_pairs={{0,6},{1,7},{2,4},{3,5},{4,2},{5,3},{6,0},{7,1},{8,14},{9,15},{10,... | collective-permute-start | bytes 405512 | tf_op jit(solution)/shard_map/ppermute | solution.py:496
  4.9 13.2 %collective-permute-start.7 = (f32[16,8,128]{2,1,0:T(8,128)S(1)}, f32[16,8,128]{2,1,0:T(8,128)S(1)}, u32[]{:S(2)}, u32[]{:S(2)}) collective-permute-start(f32[16,8,128]{2,1,0:T(8,128)S(1)} %get-tuple-element.45), channel_id=1, source_target_pairs={{0,2},{2,0},{4,6},{6,4},{10,12},{12,10},{16,18},{18,16},{20,22},{2... | collective-permute-start | bytes 196616 | tf_op jit(solution)/shard_map/ppermute | solution.py:420
  8.1 19.3 %collective-permute-start.10 = (f32[4,64,128]{2,1,0:T(8,128)S(1)}, f32[4,64,128]{2,1,0:T(8,128)S(1)}, u32[]{:S(2)}, u32[]{:S(2)}) collective-permute-start(f32[4,64,128]{2,1,0:T(8,128)S(1)} %collective-permute-done.9.refs_0_), channel_id=1, source_target_pairs={{0,8},{8,0},{16,24},{24,16},{1,9},{9,1},{17,25},{25,17},{2,10},{10... | collective-permute-start | bytes 393224 | tf_op jit(solution)/shard_map/ppermute | solution.py:387
  18.1 4.4 %collective-permute-start.8 = (f32[16,8,128]{2,1,0:T(8,128)S(1)}, f32[16,8,128]{2,1,0:T(8,128)S(1)}, u32[]{:S(2)}, u32[]{:S(2)}) collective-permute-start(f32[16,8,128]{2,1,0:T(8,128)S(1)} %collective-permute-done.7.refs_0_.got), channel_id=1, source_target_pairs={{0,8},{8,0},{16,24},{24,16},{1,9},{9,1},{17,25},{25,17},{2,10},{10... | collective-permute-start | bytes 196616 | tf_op jit(solution)/shard_map/ppermute | solution.py:387
  18.1 2.8 %collective-permute-start.11 = (f32[8,8,128]{2,1,0:T(8,128)S(1)}, f32[8,8,128]{2,1,0:T(8,128)S(1)}, u32[]{:S(2)}, u32[]{:S(2)}) collective-permute-start(f32[8,8,128]{2,1,0:T(8,128)S(1)} %shard_map.95), channel_id=1, source_target_pairs={{0,1},{1,0},{2,3},{3,2},{4,5},{5,4},{6,7},{7,6},{8,9},{9,8},{10,11... | collective-permute-start | bytes 98312 | tf_op jit(solution)/shard_map/ppermute | solution.py:427
  20.9 2.5 %collective-permute-start.12 = (f32[8,8,128]{2,1,0:T(8,128)S(1)}, f32[8,8,128]{2,1,0:T(8,128)S(1)}, u32[]{:S(2)}, u32[]{:S(2)}) collective-permute-start(f32[8,8,128]{2,1,0:T(8,128)S(1)} %collective-permute-done.11.refs_2_), channel_id=1, source_target_pairs={{0,8},{8,0},{16,24},{24,16},{1,9},{9,1},{17,25},{25,17},{2,10},{10... | collective-permute-start | bytes 98312 | tf_op jit(solution)/shard_map/ppermute | solution.py:387
  22.5 9.4 %collective-permute-start.2 = (f32[264,128]{1,0:T(8,128)S(1)}, f32[264,128]{1,0:T(8,128)S(1)}, u32[]{:S(2)}, u32[]{:S(2)}) collective-permute-start(f32[264,128]{1,0:T(8,128)S(1)} %get-tuple-element.38), channel_id=1, source_target_pairs={{0,5},{1,4},{2,7},{3,6},{4,1},{5,0},{6,3},{7,2},{8,13},{9,12},{10,... | collective-permute-start | bytes 405512 | tf_op jit(solution)/shard_map/ppermute | solution.py:496
  23.4 11.2 %collective-permute-start.3 = (f32[264,128]{1,0:T(8,128)S(1)}, f32[264,128]{1,0:T(8,128)S(1)}, u32[]{:S(2)}, u32[]{:S(2)}) collective-permute-start(f32[264,128]{1,0:T(8,128)S(1)} %get-tuple-element.39), channel_id=1, source_target_pairs={{0,4},{1,5},{2,6},{3,7},{4,0},{5,1},{6,2},{7,3},{8,12},{9,13},{10,... | collective-permute-start | bytes 405512 | tf_op jit(solution)/shard_map/ppermute | solution.py:496
  26.0 9.2 %collective-permute-start.4 = (f32[264,128]{1,0:T(8,128)S(1)}, f32[264,128]{1,0:T(8,128)S(1)}, u32[]{:S(2)}, u32[]{:S(2)}) collective-permute-start(f32[264,128]{1,0:T(8,128)S(1)} %get-tuple-element.40), channel_id=1, source_target_pairs={{0,3},{1,2},{2,1},{3,0},{4,7},{5,6},{6,5},{7,4},{8,11},{9,10},{10,... | collective-permute-start | bytes 405512 | tf_op jit(solution)/shard_map/ppermute | solution.py:496
  26.5 2.2 %copy-start.1 = (f32[1,17]{1,0:T(1,128)S(1)}, f32[1,17]{1,0:T(1,128)}, u32[]{:S(2)}) copy-start(f32[1,17]{1,0:T(1,128)} %kx.1) | copy-start | bytes 208
  26.5 2.2 %copy-start.2 = (f32[1,17]{1,0:T(1,128)S(1)}, f32[1,17]{1,0:T(1,128)}, u32[]{:S(2)}) copy-start(f32[1,17]{1,0:T(1,128)} %ky.1) | copy-start | bytes 208
  26.5 2.2 %copy-start.3 = (f32[1,33]{1,0:T(1,128)S(1)}, f32[1,33]{1,0:T(1,128)}, u32[]{:S(2)}) copy-start(f32[1,33]{1,0:T(1,128)} %kz.1) | copy-start | bytes 400
  26.5 11.6 %collective-permute-start.5 = (f32[264,128]{1,0:T(8,128)S(1)}, f32[264,128]{1,0:T(8,128)S(1)}, u32[]{:S(2)}, u32[]{:S(2)}) collective-permute-start(f32[264,128]{1,0:T(8,128)S(1)} %get-tuple-element.41), channel_id=1, source_target_pairs={{0,2},{1,3},{2,0},{3,1},{4,6},{5,7},{6,4},{7,5},{8,10},{9,11},{10,... | collective-permute-start | bytes 405512 | tf_op jit(solution)/shard_map/ppermute | solution.py:496
  27.3 10.8 %collective-permute-start.6 = (f32[264,128]{1,0:T(8,128)S(1)}, f32[264,128]{1,0:T(8,128)S(1)}, u32[]{:S(2)}, u32[]{:S(2)}) collective-permute-start(f32[264,128]{1,0:T(8,128)S(1)} %get-tuple-element.42), channel_id=1, source_target_pairs={{0,1},{1,0},{2,3},{3,2},{4,5},{5,4},{6,7},{7,6},{8,9},{9,8},{10,11... | collective-permute-start | bytes 405512 | tf_op jit(solution)/shard_map/ppermute | solution.py:496
  39.0 13.5 %collective-permute-start.16 = (f32[8,64,128]{2,1,0:T(8,128)S(1)}, f32[8,64,128]{2,1,0:T(8,128)S(1)}, u32[]{:S(2)}, u32[]{:S(2)}) collective-permute-start(f32[8,64,128]{2,1,0:T(8,128)S(1)} %get-tuple-element.61), channel_id=1, source_target_pairs={{0,1},{1,0},{2,3},{3,2},{4,5},{5,4},{6,7},{7,6},{8,9},{9,8},{10,11... | collective-permute-start | bytes 786440 | tf_op jit(solution)/shard_map/ppermute | solution.py:403
  39.3 3.1 %collective-permute-start.13 = (f32[16,8,128]{2,1,0:T(8,128)S(1)}, f32[16,8,128]{2,1,0:T(8,128)S(1)}, u32[]{:S(2)}, u32[]{:S(2)}) collective-permute-start(f32[16,8,128]{2,1,0:T(8,128)S(1)} %get-tuple-element.53), channel_id=1, source_target_pairs={{0,2},{2,0},{4,6},{6,4},{1,3},{3,1},{5,7},{7,5},{8,10},{10,8},{12,... | collective-permute-start | bytes 196616 | tf_op jit(solution)/shard_map/ppermute | solution.py:403
  39.6 5.3 %collective-permute-start.14 = (f32[16,8,128]{2,1,0:T(8,128)S(1)}, f32[16,8,128]{2,1,0:T(8,128)S(1)}, u32[]{:S(2)}, u32[]{:S(2)}) collective-permute-start(f32[16,8,128]{2,1,0:T(8,128)S(1)} %get-tuple-element.54), channel_id=1, source_target_pairs={{2,4},{4,2},{3,5},{5,3},{10,12},{12,10},{11,13},{13,11},{18,20},{2... | collective-permute-start | bytes 196616 | tf_op jit(solution)/shard_map/ppermute | solution.py:403
  46.0 4.0 %collective-permute-start.15 = (f32[256,128]{1,0:T(8,128)S(1)}, f32[256,128]{1,0:T(8,128)S(1)}, u32[]{:S(2)}, u32[]{:S(2)}) collective-permute-start(f32[256,128]{1,0:T(8,128)S(1)} %get-tuple-element.59), channel_id=1, source_target_pairs={{0,8},{8,0},{16,24},{24,16},{1,9},{9,1},{17,25},{25,17},{2,10},{10... | collective-permute-start | bytes 393224 | tf_op jit(solution)/shard_map/ppermute | solution.py:387
  49.0 3.6 %collective-permute-start.17 = (f32[2,8,8,128]{3,2,1,0:T(8,128)S(1)}, f32[2,8,8,128]{3,2,1,0:T(8,128)S(1)}, u32[]{:S(2)}, u32[]{:S(2)}) collective-permute-start(f32[2,8,8,128]{3,2,1,0:T(8,128)S(1)} %shard_map.99), channel_id=1, source_target_pairs={{0,1},{1,0},{2,3},{3,2},{4,5},{5,4},{6,7},{7,6},{8,9},{9,8},{10,11... | collective-permute-start | bytes 196616 | tf_op jit(solution)/shard_map/ppermute | solution.py:403
  53.5 2.2 %collective-permute-start.18 = (f32[256,128]{1,0:T(8,128)S(1)}, f32[256,128]{1,0:T(8,128)S(1)}, u32[]{:S(2)}, u32[]{:S(2)}) collective-permute-start(f32[256,128]{1,0:T(8,128)S(1)} %get-tuple-element.63), channel_id=1, source_target_pairs={{0,8},{8,0},{16,24},{24,16},{1,9},{9,1},{17,25},{25,17},{2,10},{10... | collective-permute-start | bytes 393224 | tf_op jit(solution)/shard_map/ppermute | solution.py:387
  54.5 5.0 %collective-permute-start.20 = (f32[256,128]{1,0:T(8,128)S(1)}, f32[256,128]{1,0:T(8,128)S(1)}, u32[]{:S(2)}, u32[]{:S(2)}) collective-permute-start(f32[256,128]{1,0:T(8,128)S(1)} %mul.28.after), channel_id=1, source_target_pairs={{0,16},{8,24},{16,0},{24,8},{1,17},{9,25},{17,1},{25,9},{2,18},{10... | collective-permute-start | bytes 393224 | tf_op jit(solution)/shard_map/ppermute | solution.py:387
  55.7 6.6 %collective-permute-start.19 = (f32[256,128]{1,0:T(8,128)S(1)}, f32[256,128]{1,0:T(8,128)S(1)}, u32[]{:S(2)}, u32[]{:S(2)}) collective-permute-start(f32[256,128]{1,0:T(8,128)S(1)} %mul.29), channel_id=1, source_target_pairs={{0,16},{8,24},{16,0},{24,8},{1,17},{9,25},{17,1},{25,9},{2,18},{10... | collective-permute-start | bytes 393224 | tf_op jit(solution)/shard_map/ppermute | solution.py:387
  59.5 3.8 %collective-permute-start.22 = (f32[256,128]{1,0:T(8,128)S(1)}, f32[256,128]{1,0:T(8,128)S(1)}, u32[]{:S(2)}, u32[]{:S(2)}) collective-permute-start(f32[256,128]{1,0:T(8,128)S(1)} %bitcast_multiply_fusion.1), channel_id=1, source_target_pairs={{0,8},{8,0},{16,24},{24,16},{1,9},{9,1},{17,25},{25,17},{2,10},{10... | collective-permute-start | bytes 393224 | tf_op jit(solution)/shard_map/ppermute | solution.py:387
  62.3 2.4 %collective-permute-start.21 = (f32[256,128]{1,0:T(8,128)S(1)}, f32[256,128]{1,0:T(8,128)S(1)}, u32[]{:S(2)}, u32[]{:S(2)}) collective-permute-start(f32[256,128]{1,0:T(8,128)S(1)} %bitcast_multiply_fusion), channel_id=1, source_target_pairs={{0,8},{8,0},{16,24},{24,16},{1,9},{9,1},{17,25},{25,17},{2,10},{10... | collective-permute-start | bytes 393224 | tf_op jit(solution)/shard_map/ppermute | solution.py:387

commit v3 on v2

--- a/solution.py
+++ b/solution.py
@@ -209,11 +209,11 @@
         lines[base + y + 1] = both[:, CZ:]
 
 
-def smear_yz(lines, base, taps, band_z, held):
+def smear_yz(lines, base, taps, band_z, held, first=0, width=CX):
     tap = [taps[i : i + 1, :] for i in range(TAPS)]
 
     def tile(t, carry):
-        at = pl.ds(pl.multiple_of(t * 8, 8), 8)
+        at = pl.ds(pl.multiple_of(first + t * 8, 8), 8)
         acc = [None] * HY
         for i in range(HY + 2 * R):
             value = lines[base + i, at, :]
@@ -222,13 +222,13 @@
                     term = tap[i - y] * value
                     acc[y] = term if acc[y] is None else acc[y] + term
         for y in range(HY):
-            held[y, at, :] = acc[y]
+            held[y, pl.ds(pl.multiple_of(t * 8, 8), 8), :] = acc[y]
         return carry
 
-    lax.fori_loop(0, CX // 8, tile, 0)
-    high, low = two(held[...].reshape(HY * CX, CZ))
+    lax.fori_loop(0, width // 8, tile, 0)
+    high, low = two(held[:, :width, :].reshape(HY * width, CZ))
     result = mm(jnp.concatenate([high, high, low], axis=1), band_z[...])
-    return [result[y * CX : (y + 1) * CX] for y in range(HY)]
+    return [result[y * width : (y + 1) * width] for y in range(HY)]
 
 
 def put_x(xa, xb, padded, count, shared=False):
@@ -290,31 +290,34 @@
         out[start + y] = value
 
 
-def put_quarters(values, mine, other, whole):
-    core = lax.axis_index("view") % 2
+def put_quarter(part, near, lines, taps, band_z, out, held):
+    core, (_, odd_y) = lax.axis_index("view") % 2, sides()
+    base = HY * (1 - odd_y if near else odd_y)
+    start = HX * (1 - core if part else core)
+    values = smear_yz(lines, base, taps, band_z, held, start, HX)
     for y in range(HY):
-        whole[pl.ds(y, CX, stride=HY), :] = values[y]
-    rows = HX * HY
-    other[...] = whole[pl.ds(pl.multiple_of((1 - core) * rows, rows), rows), :]
-    mine[...] = whole[pl.ds(pl.multiple_of(core * rows, rows), rows), :]
+        out[pl.ds(y, HX, stride=HY), :] = values[y]
 
 
 def far_kernel(own, *refs):
-    ins, (mine, other, lines, padded, held, whole) = refs[:-6], refs[-6:]
+    ins, (other, lines, padded, held) = refs[:-4], refs[-4:]
     halos, (band_x, band_z, taps) = ins[:-3], ins[-3:]
-    _, odd_y = sides()
     far_lines(own, halos[-2:], halos[:-2], band_x, padded, lines)
-    values = smear_yz(lines, HY * odd_y, taps, band_z, held)
-    put_quarters(values, mine, other, whole)
+    put_quarter(1, False, lines, taps, band_z, other, held)
 
 
 def near_kernel(after, before, *refs):
-    halos, (band_x, band_z, taps, mine, other, padded, held, whole, lines) = refs[:2], refs[2:]
-    _, odd_y = sides()
+    halos, (band_x, band_z, taps, other, lines, padded, held) = refs[:2], refs[2:]
     lines[R : R + CY] = before[R : R + CY]
     near_lines(halos, band_x, padded, lines)
-    values = smear_yz(lines, HY * (1 - odd_y), taps, band_z, held)
-    put_quarters(values, mine, other, whole)
+    put_quarter(1, True, lines, taps, band_z, other, held)
+
+
+def rest(near, lines, band_z, taps, held):
+    def kernel(lines, band_z, taps, out, held):
+        put_quarter(0, near, lines, taps, band_z, out, held)
+
+    return call(kernel, [(HX * HY, CZ)], [held], [VM] * 3)(lines, band_z, taps)[0]
 
 
 def ratio_kernel(chunks, *refs):
@@ -334,7 +337,8 @@
     def gathered(values):
         return sum(mm(chooser, part) for part in two(values))
 
-    cover = gathered(keep)
+    both = mm(chooser, jnp.concatenate(two(keep), axis=1))
+    cover = both[:, :CZ] + both[:, CZ:]
     for j in range(0, YP, 2):
         values = jnp.concatenate(
             [
@@ -471,7 +475,6 @@
     brick, half = (CY, CX, CZ), (HY, CX, CZ)
     quarter, lines = (HX * HY, CZ), (CY + 2 * R, CX, CZ)
     padded, held = pltpu.VMEM((CY, XE, CZ), F32), pltpu.VMEM((HY, CX, CZ), F32)
-    whole = pltpu.VMEM((CX * HY, CZ), F32)
 
     if bricks * GROUP == 2 * PIECES:
         room = [pltpu.VMEM((PIECES, PV), F32)]
@@ -529,10 +532,10 @@
     )
     around = halo(edges)
     near_halos, far_halos = around[:2], around[2:]
-    mine, other, before = call(
+    other, before = call(
         far_kernel,
-        [quarter, quarter, lines],
-        [padded, held, whole],
+        [quarter, lines],
+        [padded, held],
         [VM] * (len(far_halos) + 4),
     )(ratio, *far_halos, *bands)
     core, odd_y = lax.axis_index("view") % 2, lax.axis_index("by") % 2
@@ -546,15 +549,15 @@
         mine = mine * across * own.reshape(HX * HY, CZ)
         return mine, swap(mine, "view", 1)
 
-    mine = paired(mine, other)
-    work = [padded, held, whole, pltpu.VMEM(lines, F32)]
-    near = call(near_kernel, [quarter, quarter], work, [ANY] + [VM] * 6)(
+    mine = paired(rest(False, before, *bands[1:], held), other)
+    other, after = call(near_kernel, [quarter, lines], [padded, held], [ANY] + [VM] * 6)(
         mine, before, *near_halos, *bands
     )
     far_mine, far_other = product(mine, odd_y, estimate)
     updated = store([(0, False), (1, False)], [far_mine, far_other], None)
     estimate, far_mine = lax.optimization_barrier((estimate, far_mine))
-    near_mine, near_other = product(paired(*near), 1 - odd_y, estimate)
+    mine = paired(rest(True, after, *bands[1:], held), other)
+    near_mine, near_other = product(mine, 1 - odd_y, estimate)
     updated = store([(0, True)], [near_mine], updated)
     return store([(1, True)], [near_other], updated)
 

time: 65.6 us -> 64.9 us (0.989)
    pallas_call x2 -> x4, Pallas kernels: 1.96 us -> 2.13 us  [the longest x2 0.78 us: rest(): call(kernel, [(HX * HY, CZ)], [held], [VM] * 3)(lines, band_z, taps)[0]]
where the time goes in v3:
time: 64.9 us; the launch traced here: 64.7 us
  starting transfers between devices  28.1 us (43%)
  waiting for transfers between devices  26 us (40%)
  Pallas kernels  10.4 us (16%)
    ppermute x9, starting transfers between devices, swap(): lax.ppermute(x, axis, [(i, i ^ mask) for i in range(lax.axis_size(axis))])  12.4 us
    ppermute x1, waiting for transfers between devices, shared_halo(): got_x = lax.ppermute(edge_x, ('view', 'bx'), moves)  7.64 us
    ppermute x7, starting transfers between devices, local(): chunks.append(lax.ppermute(packed[s], ('bx', 'by'), pair))  6.72 us
    ppermute x7, waiting for transfers between devices, local(): chunks.append(lax.ppermute(packed[s], ('bx', 'by'), pair))  6.16 us
    ppermute x9, waiting for transfers between devices, swap(): lax.ppermute(x, axis, [(i, i ^ mask) for i in range(lax.axis_size(axis))])  5.41 us
    ppermute x4, waiting for transfers between devices, move(): return lax.ppermute(value, axis, moves) if moves else jnp.zeros_like(value)  5.35 us
    ppermute x1, starting transfers between devices, shared_halo(): got_x = lax.ppermute(edge_x, ('view', 'bx'), moves)  3.2 us
    ppermute x4, starting transfers between devices, move(): return lax.ppermute(value, axis, moves) if moves else jnp.zeros_like(value)  3.1 us
  transfers between devices with their start and end apart: 23, of which 12 were waited for; matrix products, arithmetic and copies ran while one was open for 0% of the time, Pallas kernels for 9%

profile of v3, /device:TPU:9, one launch (start us, length us, event | category | flops | bytes accessed | tf_op | source)
XLA Modules:
  0.0 64.7 jit_solution(5586329709418799918)
XLA Ops:
  0.0 1.9 %shard_map.91 = (f32[264,128]{1,0:T(8,128)S(1)}, f32[264,128]{1,0:T(8,128)S(1)}, f32[264,128]{1,0:T(8,128)S(1)}, f32[264,128]{1,0:T(8,128)S(1)}, f32[264,128]{1,...) custom-call(f32[256,512]{1,0:T(8,128)} %bitcast.16, ...), custom_call_target="tpu_custom_call" | custom-call | flops 4194304 | bytes 1048576 | tf_op jit(solution)/shard_map/pallas_call | solution.py:484
  2.2 1.3 %collective-permute-start.9 = (f32[4,64,128]{2,1,0:T(8,128)S(1)}, f32[4,64,128]{2,1,0:T(8,128)S(1)}, u32[]{:S(2)}, u32[]{:S(2)}) collective-permute-start(f32[4,64,128]{2,1,0:T(8,128)S(1)} %get-tuple-element.50), channel_id=1, source_target_pairs={{0,1},{1,0},{2,3},{3,2},{4,5},{5,4},{6,7},{7,6},{8,9},{9,8},{10,11... | collective-permute-start | bytes 393224 | tf_op jit(solution)/shard_map/ppermute | solution.py:427
  3.5 1.2 %collective-permute-start = (f32[264,128]{1,0:T(8,128)S(1)}, f32[264,128]{1,0:T(8,128)S(1)}, u32[]{:S(2)}, u32[]{:S(2)}) collective-permute-start(f32[264,128]{1,0:T(8,128)S(1)} %get-tuple-element.35), channel_id=1, source_target_pairs={{0,7},{1,6},{2,5},{3,4},{4,3},{5,2},{6,1},{7,0},{8,15},{9,14},{10,... | collective-permute-start | bytes 405512 | tf_op jit(solution)/shard_map/ppermute | solution.py:499
  4.9 3.2 %collective-permute-start.7 = (f32[16,8,128]{2,1,0:T(8,128)S(1)}, f32[16,8,128]{2,1,0:T(8,128)S(1)}, u32[]{:S(2)}, u32[]{:S(2)}) collective-permute-start(f32[16,8,128]{2,1,0:T(8,128)S(1)} %get-tuple-element.44), channel_id=1, source_target_pairs={{0,2},{2,0},{4,6},{6,4},{10,12},{12,10},{16,18},{18,16},{20,22},{2... | collective-permute-start | bytes 196616 | tf_op jit(solution)/shard_map/ppermute | solution.py:424
  8.1 2.4 %collective-permute-start.10 = (f32[4,64,128]{2,1,0:T(8,128)S(1)}, f32[4,64,128]{2,1,0:T(8,128)S(1)}, u32[]{:S(2)}, u32[]{:S(2)}) collective-permute-start(f32[4,64,128]{2,1,0:T(8,128)S(1)} %collective-permute-done.9.refs_0_), channel_id=1, source_target_pairs={{0,8},{8,0},{16,24},{24,16},{1,9},{9,1},{17,25},{25,17},{2,10},{10... | collective-permute-start | bytes 393224 | tf_op jit(solution)/shard_map/ppermute | solution.py:391
  10.4 7.6 %collective-permute-done.7.refs_0_.got = f32[16,8,128]{2,1,0:T(8,128)S(1)} collective-permute-done((f32[16,8,128]{2,1,0:T(8,128)S(1)}, f32[16,8,128]{2,1,0:T(8,128)S(1)}, u32[]{:S(2)}, u32[]{:S(2)}) %collective-permute-start.7) | collective-permute-done | bytes 65568 | tf_op jit(solution)/shard_map/ppermute | solution.py:424
  18.1 1.4 %collective-permute-start.11 = (f32[8,8,128]{2,1,0:T(8,128)S(1)}, f32[8,8,128]{2,1,0:T(8,128)S(1)}, u32[]{:S(2)}, u32[]{:S(2)}) collective-permute-start(f32[8,8,128]{2,1,0:T(8,128)S(1)} %shard_map.95), channel_id=1, source_target_pairs={{0,1},{1,0},{2,3},{3,2},{4,5},{5,4},{6,7},{7,6},{8,9},{9,8},{10,11... | collective-permute-start | bytes 98312 | tf_op jit(solution)/shard_map/ppermute | solution.py:431
  19.5 1.4 %collective-permute-done.11.refs_2_ = f32[8,8,128]{2,1,0:T(8,128)S(1)} collective-permute-done((f32[8,8,128]{2,1,0:T(8,128)S(1)}, f32[8,8,128]{2,1,0:T(8,128)S(1)}, u32[]{:S(2)}, u32[]{:S(2)}) %collective-permute-start.11) | collective-permute-done | bytes 32800 | tf_op jit(solution)/shard_map/ppermute | solution.py:431
  20.9 1.7 %collective-permute-start.12 = (f32[8,8,128]{2,1,0:T(8,128)S(1)}, f32[8,8,128]{2,1,0:T(8,128)S(1)}, u32[]{:S(2)}, u32[]{:S(2)}) collective-permute-start(f32[8,8,128]{2,1,0:T(8,128)S(1)} %collective-permute-done.11.refs_2_), channel_id=1, source_target_pairs={{0,8},{8,0},{16,24},{24,16},{1,9},{9,1},{17,25},{25,17},{2,10},{10... | collective-permute-start | bytes 98312 | tf_op jit(solution)/shard_map/ppermute | solution.py:391
  22.5 0.9 %collective-permute-done.12.refs_3_ = f32[8,8,128]{2,1,0:T(8,128)S(1)} collective-permute-done((f32[8,8,128]{2,1,0:T(8,128)S(1)}, f32[8,8,128]{2,1,0:T(8,128)S(1)}, u32[]{:S(2)}, u32[]{:S(2)}) %collective-permute-start.12) | collective-permute-done | bytes 32800 | tf_op jit(solution)/shard_map/ppermute | solution.py:391
  23.4 2.6 %collective-permute-start.3 = (f32[264,128]{1,0:T(8,128)S(1)}, f32[264,128]{1,0:T(8,128)S(1)}, u32[]{:S(2)}, u32[]{:S(2)}) collective-permute-start(f32[264,128]{1,0:T(8,128)S(1)} %get-tuple-element.38), channel_id=1, source_target_pairs={{0,4},{1,5},{2,6},{3,7},{4,0},{5,1},{6,2},{7,3},{8,12},{9,13},{10,... | collective-permute-start | bytes 405512 | tf_op jit(solution)/shard_map/ppermute | solution.py:499
  26.5 0.8 %collective-permute-start.5 = (f32[264,128]{1,0:T(8,128)S(1)}, f32[264,128]{1,0:T(8,128)S(1)}, u32[]{:S(2)}, u32[]{:S(2)}) collective-permute-start(f32[264,128]{1,0:T(8,128)S(1)} %get-tuple-element.40), channel_id=1, source_target_pairs={{0,2},{1,3},{2,0},{3,1},{4,6},{5,7},{6,4},{7,5},{8,10},{9,11},{10,... | collective-permute-start | bytes 405512 | tf_op jit(solution)/shard_map/ppermute | solution.py:499
  27.3 1.4 %collective-permute-start.6 = (f32[264,128]{1,0:T(8,128)S(1)}, f32[264,128]{1,0:T(8,128)S(1)}, u32[]{:S(2)}, u32[]{:S(2)}) collective-permute-start(f32[264,128]{1,0:T(8,128)S(1)} %get-tuple-element.41), channel_id=1, source_target_pairs={{0,1},{1,0},{2,3},{3,2},{4,5},{5,4},{6,7},{7,6},{8,9},{9,8},{10,11... | collective-permute-start | bytes 405512 | tf_op jit(solution)/shard_map/ppermute | solution.py:499
  28.7 1.2 %shard_map.93 = (bf16[64,240]{1,0:T(8,128)(2,1)S(1)}, bf16[384,128]{1,0:T(8,128)(2,1)S(1)}, f32[24,128]{1,0:T(8,128)S(1)}, bf16[64,240]{1,0:T(8,128)(2,1)S(1)}, ...) custom-call(f32[1,17]{1,0:T(1,128)S(1)} %copy-done.1, f32[1,17]{1,0:T(1,128)S(1)} %copy-done.2, f32[1,33]{1,0:T(1,128)S(1)} %copy-done.3), custom_call_target="tpu_custom_call" | custom-call | flops 4194304 | bytes 1048576 | tf_op jit(solution)/shard_map/pallas_call | solution.py:516
  30.0 1.0 %shard_map.94 = (f32[8,64,128]{2,1,0:T(8,128)S(1)}, f32[32,64,128]{2,1,0:T(8,128)S(1)}) custom-call(f32[16,64,128]{2,1,0:T(8,128)S(1)} %get-tuple-element.43.own, f32[16,8,128]{2,1,0:T(8,128)S(1)} %collective-permute-done.7.refs_0_.got, f32[16,8,128]{2,1,0:T(8,128)S(1)} %collective-permute-done.8.refs_1_, ...), custom_call_target="tpu_custom_call" | custom-call | flops 4194304 | bytes 1048576 | tf_op jit(solution)/shard_map/pallas_call | solution.py:519
  31.0 1.0 %shard_map.96.refs_8_ = f32[16,64,128]{2,1,0:T(8,128)S(1)} custom-call(f32[8,64,128]{2,1,0:T(8,128)S(1)} %get-tuple-element.48.far, f32[32,64,128]{2,1,0:T(8,128)S(1)} %get-tuple-element.49.before, f32[4,64,128]{2,1,0:T(8,128)S(1)} %collective-permute-done.9.refs_0_, f32[4,64,128]{2,1,0:T(8,128)S(1)} %collective-permute-done.10.refs_1_, ...), custom_call_target="tpu_custom_call" | custom-call | flops 4194304 | bytes 1048576 | tf_op jit(solution)/shard_map/pallas_call | solution.py:523
  32.0 2.7 %collective-permute-done.3.refs_4_ = f32[264,128]{1,0:T(8,128)S(1)} collective-permute-done((f32[264,128]{1,0:T(8,128)S(1)}, f32[264,128]{1,0:T(8,128)S(1)}, u32[]{:S(2)}, u32[]{:S(2)}) %collective-permute-start.3) | collective-permute-done | bytes 135200 | tf_op jit(solution)/shard_map/ppermute | solution.py:499
  35.2 2.9 %collective-permute-done.5.refs_6_ = f32[264,128]{1,0:T(8,128)S(1)} collective-permute-done((f32[264,128]{1,0:T(8,128)S(1)}, f32[264,128]{1,0:T(8,128)S(1)}, u32[]{:S(2)}, u32[]{:S(2)}) %collective-permute-start.5) | collective-permute-done | bytes 135200 | tf_op jit(solution)/shard_map/ppermute | solution.py:499
  38.1 0.8 %shard_map.97 = (f32[16,64,128]{2,1,0:T(8,128)S(1)}, f32[8,64,128]{2,1,0:T(8,128)S(1)}, f32[16,8,128]{2,1,0:T(8,128)S(1)}, f32[16,8,128]{2,1,0:T(8,128)S(1)}) custom-call(f32[264,128]{1,0:T(8,128)S(1)} %get-tuple-element.34.refs_0_, f32[264,128]{1,0:T(8,128)S(1)} %collective-permute-done.refs_1_, f32[264,128]{1,0:T(8,128)S(1)} %collective-permute-done.1.refs_2_, ...), custom_call_target="tpu_custom_call" | custom-call | flops 4194304 | bytes 1048576 | tf_op jit(solution)/shard_map/pallas_call | solution.py:530
  39.5 2.5 %collective-permute-start.14 = (f32[16,8,128]{2,1,0:T(8,128)S(1)}, f32[16,8,128]{2,1,0:T(8,128)S(1)}, u32[]{:S(2)}, u32[]{:S(2)}) collective-permute-start(f32[16,8,128]{2,1,0:T(8,128)S(1)} %get-tuple-element.53), channel_id=1, source_target_pairs={{2,4},{4,2},{3,5},{5,3},{10,12},{12,10},{11,13},{13,11},{18,20},{2... | collective-permute-start | bytes 196616 | tf_op jit(solution)/shard_map/ppermute | solution.py:407
  42.4 2.5 %collective-permute-done.14.refs_1_.xb = f32[16,8,128]{2,1,0:T(8,128)S(1)} collective-permute-done((f32[16,8,128]{2,1,0:T(8,128)S(1)}, f32[16,8,128]{2,1,0:T(8,128)S(1)}, u32[]{:S(2)}, u32[]{:S(2)}) %collective-permute-start.14) | collective-permute-done | bytes 65568 | tf_op jit(solution)/shard_map/ppermute | solution.py:407
  44.8 0.7 %shard_map.98 = (f32[256,128]{1,0:T(8,128)S(1)}, f32[32,64,128]{2,1,0:T(8,128)S(1)}) custom-call(f32[16,64,128]{2,1,0:T(8,128)S(1)} %get-tuple-element.51.own, f32[16,8,128]{2,1,0:T(8,128)S(1)} %collective-permute-done.13.refs_0_.xa, f32[16,8,128]{2,1,0:T(8,128)S(1)} %collective-permute-done.14.refs_1_.xb, bf16[64,240]{1,0:T(8,128)(2,1)S(1)} %get-tuple-element.54.refs_2_, ...), custom_call_target="tpu_custom_call" | custom-call | flops 4194304 | bytes 1048576 | tf_op jit(solution)/shard_map/pallas_call | solution.py:535
  45.6 3.0 %collective-permute-start.15 = (f32[256,128]{1,0:T(8,128)S(1)}, f32[256,128]{1,0:T(8,128)S(1)}, u32[]{:S(2)}, u32[]{:S(2)}) collective-permute-start(f32[256,128]{1,0:T(8,128)S(1)} %get-tuple-element.58), channel_id=1, source_target_pairs={{0,8},{8,0},{16,24},{24,16},{1,9},{9,1},{17,25},{25,17},{2,10},{10... | collective-permute-start | bytes 393224 | tf_op jit(solution)/shard_map/ppermute | solution.py:391
  49.6 2.6 %collective-permute-done.17.refs_1_ = f32[2,8,8,128]{3,2,1,0:T(8,128)S(1)} collective-permute-done((f32[2,8,8,128]{3,2,1,0:T(8,128)S(1)}, f32[2,8,8,128]{3,2,1,0:T(8,128)S(1)}, u32[]{:S(2)}, u32[]{:S(2)}) %collective-permute-start.17) | collective-permute-done | bytes 65568 | tf_op jit(solution)/shard_map/ppermute | solution.py:407
  52.8 1.0 %collective-permute-start.18 = (f32[256,128]{1,0:T(8,128)S(1)}, f32[256,128]{1,0:T(8,128)S(1)}, u32[]{:S(2)}, u32[]{:S(2)}) collective-permute-start(f32[256,128]{1,0:T(8,128)S(1)} %get-tuple-element.61), channel_id=1, source_target_pairs={{0,8},{8,0},{16,24},{24,16},{1,9},{9,1},{17,25},{25,17},{2,10},{10... | collective-permute-start | bytes 393224 | tf_op jit(solution)/shard_map/ppermute | solution.py:391
  53.8 1.2 %collective-permute-start.20 = (f32[256,128]{1,0:T(8,128)S(1)}, f32[256,128]{1,0:T(8,128)S(1)}, u32[]{:S(2)}, u32[]{:S(2)}) collective-permute-start(f32[256,128]{1,0:T(8,128)S(1)} %mul.28.after), channel_id=1, source_target_pairs={{0,16},{8,24},{16,0},{24,8},{1,17},{9,25},{17,1},{25,9},{2,18},{10... | collective-permute-start | bytes 393224 | tf_op jit(solution)/shard_map/ppermute | solution.py:391
  56.1 2.7 %collective-permute-done.20 = f32[256,128]{1,0:T(8,128)S(1)} collective-permute-done((f32[256,128]{1,0:T(8,128)S(1)}, f32[256,128]{1,0:T(8,128)S(1)}, u32[]{:S(2)}, u32[]{:S(2)}) %collective-permute-start.20) | collective-permute-done | bytes 131104 | tf_op jit(solution)/shard_map/ppermute | solution.py:391
  58.8 1.5 %collective-permute-start.22 = (f32[256,128]{1,0:T(8,128)S(1)}, f32[256,128]{1,0:T(8,128)S(1)}, u32[]{:S(2)}, u32[]{:S(2)}) collective-permute-start(f32[256,128]{1,0:T(8,128)S(1)} %bitcast_multiply_fusion.1), channel_id=1, source_target_pairs={{0,8},{8,0},{16,24},{24,16},{1,9},{9,1},{17,25},{25,17},{2,10},{10... | collective-permute-start | bytes 393224 | tf_op jit(solution)/shard_map/ppermute | solution.py:391
  60.4 1.2 %collective-permute-done.19 = f32[256,128]{1,0:T(8,128)S(1)} collective-permute-done((f32[256,128]{1,0:T(8,128)S(1)}, f32[256,128]{1,0:T(8,128)S(1)}, u32[]{:S(2)}, u32[]{:S(2)}) %collective-permute-start.19) | collective-permute-done | bytes 131104 | tf_op jit(solution)/shard_map/ppermute | solution.py:391
  61.6 1.0 %collective-permute-start.21 = (f32[256,128]{1,0:T(8,128)S(1)}, f32[256,128]{1,0:T(8,128)S(1)}, u32[]{:S(2)}, u32[]{:S(2)}) collective-permute-start(f32[256,128]{1,0:T(8,128)S(1)} %bitcast_multiply_fusion), channel_id=1, source_target_pairs={{0,8},{8,0},{16,24},{24,16},{1,9},{9,1},{17,25},{25,17},{2,10},{10... | collective-permute-start | bytes 393224 | tf_op jit(solution)/shard_map/ppermute | solution.py:391
  62.6 0.7 %shard_map.103.refs_1_ = f32[64,16,128]{2,1,0:T(8,128)} custom-call(f32[32,8,128]{2,1,0:T(8,128)S(1)} %bitcast.13, f32[32,8,128]{2,1,0:T(8,128)S(1)} %bitcast.15), custom_call_target="tpu_custom_call" | custom-call | flops 4194304 | bytes 1048576 | tf_op jit(solution)/shard_map/pallas_call | solution.py:387
  64.1 0.7 %shard_map.105 = f32[64,16,128]{2,1,0:T(8,128)} custom-call(f32[32,8,128]{2,1,0:T(8,128)S(1)} %bitcast.14, f32[64,16,128]{2,1,0:T(8,128)} %shard_map.104.refs_1_), custom_call_target="tpu_custom_call", output_to_operand_aliasing={{}: (1, {})} | custom-call | flops 4194304 | bytes 1048576 | tf_op jit(solution)/shard_map/pallas_call | solution.py:387
  (41 shorter events, 5.8 us)
Async XLA Ops:
  0.0 1.9 %copy-start = (f32[64,16,128]{2,1,0:T(8,128)S(1)}, f32[64,16,128]{2,1,0:T(8,128)}, u32[]{:S(2)}) copy-start(f32[64,16,128]{2,1,0:T(8,128)} %param.9) | copy-start | bytes 1572868
  2.2 5.9 %collective-permute-start.9 = (f32[4,64,128]{2,1,0:T(8,128)S(1)}, f32[4,64,128]{2,1,0:T(8,128)S(1)}, u32[]{:S(2)}, u32[]{:S(2)}) collective-permute-start(f32[4,64,128]{2,1,0:T(8,128)S(1)} %get-tuple-element.50), channel_id=1, source_target_pairs={{0,1},{1,0},{2,3},{3,2},{4,5},{5,4},{6,7},{7,6},{8,9},{9,8},{10,11... | collective-permute-start | bytes 393224 | tf_op jit(solution)/shard_map/ppermute | solution.py:427
  3.5 22.5 %collective-permute-start = (f32[264,128]{1,0:T(8,128)S(1)}, f32[264,128]{1,0:T(8,128)S(1)}, u32[]{:S(2)}, u32[]{:S(2)}) collective-permute-start(f32[264,128]{1,0:T(8,128)S(1)} %get-tuple-element.35), channel_id=1, source_target_pairs={{0,7},{1,6},{2,5},{3,4},{4,3},{5,2},{6,1},{7,0},{8,15},{9,14},{10,... | collective-permute-start | bytes 405512 | tf_op jit(solution)/shard_map/ppermute | solution.py:499
  4.7 21.8 %collective-permute-start.1 = (f32[264,128]{1,0:T(8,128)S(1)}, f32[264,128]{1,0:T(8,128)S(1)}, u32[]{:S(2)}, u32[]{:S(2)}) collective-permute-start(f32[264,128]{1,0:T(8,128)S(1)} %get-tuple-element.36), channel_id=1, source_target_pairs={{0,6},{1,7},{2,4},{3,5},{4,2},{5,3},{6,0},{7,1},{8,14},{9,15},{10,... | collective-permute-start | bytes 405512 | tf_op jit(solution)/shard_map/ppermute | solution.py:499
  4.9 13.2 %collective-permute-start.7 = (f32[16,8,128]{2,1,0:T(8,128)S(1)}, f32[16,8,128]{2,1,0:T(8,128)S(1)}, u32[]{:S(2)}, u32[]{:S(2)}) collective-permute-start(f32[16,8,128]{2,1,0:T(8,128)S(1)} %get-tuple-element.44), channel_id=1, source_target_pairs={{0,2},{2,0},{4,6},{6,4},{10,12},{12,10},{16,18},{18,16},{20,22},{2... | collective-permute-start | bytes 196616 | tf_op jit(solution)/shard_map/ppermute | solution.py:424
  8.1 19.3 %collective-permute-start.10 = (f32[4,64,128]{2,1,0:T(8,128)S(1)}, f32[4,64,128]{2,1,0:T(8,128)S(1)}, u32[]{:S(2)}, u32[]{:S(2)}) collective-permute-start(f32[4,64,128]{2,1,0:T(8,128)S(1)} %collective-permute-done.9.refs_0_), channel_id=1, source_target_pairs={{0,8},{8,0},{16,24},{24,16},{1,9},{9,1},{17,25},{25,17},{2,10},{10... | collective-permute-start | bytes 393224 | tf_op jit(solution)/shard_map/ppermute | solution.py:391
  18.1 4.4 %collective-permute-start.8 = (f32[16,8,128]{2,1,0:T(8,128)S(1)}, f32[16,8,128]{2,1,0:T(8,128)S(1)}, u32[]{:S(2)}, u32[]{:S(2)}) collective-permute-start(f32[16,8,128]{2,1,0:T(8,128)S(1)} %collective-permute-done.7.refs_0_.got), channel_id=1, source_target_pairs={{0,8},{8,0},{16,24},{24,16},{1,9},{9,1},{17,25},{25,17},{2,10},{10... | collective-permute-start | bytes 196616 | tf_op jit(solution)/shard_map/ppermute | solution.py:391
  18.1 2.8 %collective-permute-start.11 = (f32[8,8,128]{2,1,0:T(8,128)S(1)}, f32[8,8,128]{2,1,0:T(8,128)S(1)}, u32[]{:S(2)}, u32[]{:S(2)}) collective-permute-start(f32[8,8,128]{2,1,0:T(8,128)S(1)} %shard_map.95), channel_id=1, source_target_pairs={{0,1},{1,0},{2,3},{3,2},{4,5},{5,4},{6,7},{7,6},{8,9},{9,8},{10,11... | collective-permute-start | bytes 98312 | tf_op jit(solution)/shard_map/ppermute | solution.py:431
  20.9 2.5 %collective-permute-start.12 = (f32[8,8,128]{2,1,0:T(8,128)S(1)}, f32[8,8,128]{2,1,0:T(8,128)S(1)}, u32[]{:S(2)}, u32[]{:S(2)}) collective-permute-start(f32[8,8,128]{2,1,0:T(8,128)S(1)} %collective-permute-done.11.refs_2_), channel_id=1, source_target_pairs={{0,8},{8,0},{16,24},{24,16},{1,9},{9,1},{17,25},{25,17},{2,10},{10... | collective-permute-start | bytes 98312 | tf_op jit(solution)/shard_map/ppermute | solution.py:391
  22.5 9.4 %collective-permute-start.2 = (f32[264,128]{1,0:T(8,128)S(1)}, f32[264,128]{1,0:T(8,128)S(1)}, u32[]{:S(2)}, u32[]{:S(2)}) collective-permute-start(f32[264,128]{1,0:T(8,128)S(1)} %get-tuple-element.37), channel_id=1, source_target_pairs={{0,5},{1,4},{2,7},{3,6},{4,1},{5,0},{6,3},{7,2},{8,13},{9,12},{10,... | collective-permute-start | bytes 405512 | tf_op jit(solution)/shard_map/ppermute | solution.py:499
  23.4 11.2 %collective-permute-start.3 = (f32[264,128]{1,0:T(8,128)S(1)}, f32[264,128]{1,0:T(8,128)S(1)}, u32[]{:S(2)}, u32[]{:S(2)}) collective-permute-start(f32[264,128]{1,0:T(8,128)S(1)} %get-tuple-element.38), channel_id=1, source_target_pairs={{0,4},{1,5},{2,6},{3,7},{4,0},{5,1},{6,2},{7,3},{8,12},{9,13},{10,... | collective-permute-start | bytes 405512 | tf_op jit(solution)/shard_map/ppermute | solution.py:499
  26.0 9.2 %collective-permute-start.4 = (f32[264,128]{1,0:T(8,128)S(1)}, f32[264,128]{1,0:T(8,128)S(1)}, u32[]{:S(2)}, u32[]{:S(2)}) collective-permute-start(f32[264,128]{1,0:T(8,128)S(1)} %get-tuple-element.39), channel_id=1, source_target_pairs={{0,3},{1,2},{2,1},{3,0},{4,7},{5,6},{6,5},{7,4},{8,11},{9,10},{10,... | collective-permute-start | bytes 405512 | tf_op jit(solution)/shard_map/ppermute | solution.py:499
  26.5 2.2 %copy-start.1 = (f32[1,17]{1,0:T(1,128)S(1)}, f32[1,17]{1,0:T(1,128)}, u32[]{:S(2)}) copy-start(f32[1,17]{1,0:T(1,128)} %kx.1) | copy-start | bytes 208
  26.5 2.2 %copy-start.2 = (f32[1,17]{1,0:T(1,128)S(1)}, f32[1,17]{1,0:T(1,128)}, u32[]{:S(2)}) copy-start(f32[1,17]{1,0:T(1,128)} %ky.1) | copy-start | bytes 208
  26.5 2.2 %copy-start.3 = (f32[1,33]{1,0:T(1,128)S(1)}, f32[1,33]{1,0:T(1,128)}, u32[]{:S(2)}) copy-start(f32[1,33]{1,0:T(1,128)} %kz.1) | copy-start | bytes 400
  26.5 11.6 %collective-permute-start.5 = (f32[264,128]{1,0:T(8,128)S(1)}, f32[264,128]{1,0:T(8,128)S(1)}, u32[]{:S(2)}, u32[]{:S(2)}) collective-permute-start(f32[264,128]{1,0:T(8,128)S(1)} %get-tuple-element.40), channel_id=1, source_target_pairs={{0,2},{1,3},{2,0},{3,1},{4,6},{5,7},{6,4},{7,5},{8,10},{9,11},{10,... | collective-permute-start | bytes 405512 | tf_op jit(solution)/shard_map/ppermute | solution.py:499
  27.3 10.8 %collective-permute-start.6 = (f32[264,128]{1,0:T(8,128)S(1)}, f32[264,128]{1,0:T(8,128)S(1)}, u32[]{:S(2)}, u32[]{:S(2)}) collective-permute-start(f32[264,128]{1,0:T(8,128)S(1)} %get-tuple-element.41), channel_id=1, source_target_pairs={{0,1},{1,0},{2,3},{3,2},{4,5},{5,4},{6,7},{7,6},{8,9},{9,8},{10,11... | collective-permute-start | bytes 405512 | tf_op jit(solution)/shard_map/ppermute | solution.py:499
  38.9 13.2 %collective-permute-start.16 = (f32[8,64,128]{2,1,0:T(8,128)S(1)}, f32[8,64,128]{2,1,0:T(8,128)S(1)}, u32[]{:S(2)}, u32[]{:S(2)}) collective-permute-start(f32[8,64,128]{2,1,0:T(8,128)S(1)} %get-tuple-element.59), channel_id=1, source_target_pairs={{0,1},{1,0},{2,3},{3,2},{4,5},{5,4},{6,7},{7,6},{8,9},{9,8},{10,11... | collective-permute-start | bytes 786440 | tf_op jit(solution)/shard_map/ppermute | solution.py:407
  39.2 3.1 %collective-permute-start.13 = (f32[16,8,128]{2,1,0:T(8,128)S(1)}, f32[16,8,128]{2,1,0:T(8,128)S(1)}, u32[]{:S(2)}, u32[]{:S(2)}) collective-permute-start(f32[16,8,128]{2,1,0:T(8,128)S(1)} %get-tuple-element.52), channel_id=1, source_target_pairs={{0,2},{2,0},{4,6},{6,4},{1,3},{3,1},{5,7},{7,5},{8,10},{10,8},{12,... | collective-permute-start | bytes 196616 | tf_op jit(solution)/shard_map/ppermute | solution.py:407
  39.5 5.3 %collective-permute-start.14 = (f32[16,8,128]{2,1,0:T(8,128)S(1)}, f32[16,8,128]{2,1,0:T(8,128)S(1)}, u32[]{:S(2)}, u32[]{:S(2)}) collective-permute-start(f32[16,8,128]{2,1,0:T(8,128)S(1)} %get-tuple-element.53), channel_id=1, source_target_pairs={{2,4},{4,2},{3,5},{5,3},{10,12},{12,10},{11,13},{13,11},{18,20},{2... | collective-permute-start | bytes 196616 | tf_op jit(solution)/shard_map/ppermute | solution.py:407
  45.6 4.0 %collective-permute-start.15 = (f32[256,128]{1,0:T(8,128)S(1)}, f32[256,128]{1,0:T(8,128)S(1)}, u32[]{:S(2)}, u32[]{:S(2)}) collective-permute-start(f32[256,128]{1,0:T(8,128)S(1)} %get-tuple-element.58), channel_id=1, source_target_pairs={{0,8},{8,0},{16,24},{24,16},{1,9},{9,1},{17,25},{25,17},{2,10},{10... | collective-permute-start | bytes 393224 | tf_op jit(solution)/shard_map/ppermute | solution.py:391
  48.6 3.6 %collective-permute-start.17 = (f32[2,8,8,128]{3,2,1,0:T(8,128)S(1)}, f32[2,8,8,128]{3,2,1,0:T(8,128)S(1)}, u32[]{:S(2)}, u32[]{:S(2)}) collective-permute-start(f32[2,8,8,128]{3,2,1,0:T(8,128)S(1)} %shard_map.100), channel_id=1, source_target_pairs={{0,1},{1,0},{2,3},{3,2},{4,5},{5,4},{6,7},{7,6},{8,9},{9,8},{10,11... | collective-permute-start | bytes 196616 | tf_op jit(solution)/shard_map/ppermute | solution.py:407
  52.8 2.6 %collective-permute-start.18 = (f32[256,128]{1,0:T(8,128)S(1)}, f32[256,128]{1,0:T(8,128)S(1)}, u32[]{:S(2)}, u32[]{:S(2)}) collective-permute-start(f32[256,128]{1,0:T(8,128)S(1)} %get-tuple-element.61), channel_id=1, source_target_pairs={{0,8},{8,0},{16,24},{24,16},{1,9},{9,1},{17,25},{25,17},{2,10},{10... | collective-permute-start | bytes 393224 | tf_op jit(solution)/shard_map/ppermute | solution.py:391
  53.8 5.0 %collective-permute-start.20 = (f32[256,128]{1,0:T(8,128)S(1)}, f32[256,128]{1,0:T(8,128)S(1)}, u32[]{:S(2)}, u32[]{:S(2)}) collective-permute-start(f32[256,128]{1,0:T(8,128)S(1)} %mul.28.after), channel_id=1, source_target_pairs={{0,16},{8,24},{16,0},{24,8},{1,17},{9,25},{17,1},{25,9},{2,18},{10... | collective-permute-start | bytes 393224 | tf_op jit(solution)/shard_map/ppermute | solution.py:391
  55.4 6.2 %collective-permute-start.19 = (f32[256,128]{1,0:T(8,128)S(1)}, f32[256,128]{1,0:T(8,128)S(1)}, u32[]{:S(2)}, u32[]{:S(2)}) collective-permute-start(f32[256,128]{1,0:T(8,128)S(1)} %mul.29), channel_id=1, source_target_pairs={{0,16},{8,24},{16,0},{24,8},{1,17},{9,25},{17,1},{25,9},{2,18},{10... | collective-permute-start | bytes 393224 | tf_op jit(solution)/shard_map/ppermute | solution.py:391
  58.8 3.8 %collective-permute-start.22 = (f32[256,128]{1,0:T(8,128)S(1)}, f32[256,128]{1,0:T(8,128)S(1)}, u32[]{:S(2)}, u32[]{:S(2)}) collective-permute-start(f32[256,128]{1,0:T(8,128)S(1)} %bitcast_multiply_fusion.1), channel_id=1, source_target_pairs={{0,8},{8,0},{16,24},{24,16},{1,9},{9,1},{17,25},{25,17},{2,10},{10... | collective-permute-start | bytes 393224 | tf_op jit(solution)/shard_map/ppermute | solution.py:391
  61.6 2.4 %collective-permute-start.21 = (f32[256,128]{1,0:T(8,128)S(1)}, f32[256,128]{1,0:T(8,128)S(1)}, u32[]{:S(2)}, u32[]{:S(2)}) collective-permute-start(f32[256,128]{1,0:T(8,128)S(1)} %bitcast_multiply_fusion), channel_id=1, source_target_pairs={{0,8},{8,0},{16,24},{24,16},{1,9},{9,1},{17,25},{25,17},{2,10},{10... | collective-permute-start | bytes 393224 | tf_op jit(solution)/shard_map/ppermute | solution.py:391
